TPU v7x, 32 devices: a whole 2x2x4 slice. The times are simulated.
32 devices in a mesh: dp: 8 (over z, y), tensor: 4 (over x, core).
Axes of the slice: x: 2, y: 2, z: 4, core: 2. Of those that a mesh axis runs over, the one named last changes fastest.
Arguments:
- tokens: bfloat16 [3072, 1024], P(('dp', 'tensor')), may hold values from -6 to 6
- seq_lengths: int32 [8, 8], P('dp'), may hold values from 1 to 192, 384 in all within a row
- ln1_gain: float32 [1024], replicated, may hold values from 0.5 to 1.5
- ln1_bias: float32 [1024], replicated, may hold values from -3 to 3
- ln2_gain: float32 [1024], replicated, may hold values from 0.5 to 1.5
- ln2_bias: float32 [1024], replicated, may hold values from -3 to 3
- qkv_weight: bfloat16 [1024, 3072], P(None, 'tensor'), as said below
- qkv_bias: float32 [3072], P('tensor'), may hold values from -3 to 3
- out_weight: bfloat16 [1024, 1024], P('tensor'), may hold values from -0.75 to 0.75
- out_bias: float32 [1024], replicated, may hold values from -3 to 3
- up_weight: bfloat16 [1024, 4096], P(None, 'tensor'), may hold values from -0.1875 to 0.1875
- up_bias: float32 [4096], P('tensor'), may hold values from -3 to 3
- down_weight: bfloat16 [4096, 1024], P('tensor'), may hold values from -0.125 to 0.125
- down_bias: float32 [1024], replicated, may hold values from -3 to 3
- cotangent: bfloat16 [3072, 1024], P(('dp', 'tensor')), may hold values from -6 to 6
Outputs:
- output: bfloat16 [3072, 1024], P(('dp', 'tensor'))
- grad_input: bfloat16 [3072, 1024], P(('dp', 'tensor'))
- grad_ln1_gain: float32 [1024], replicated
- grad_ln1_bias: float32 [1024], replicated
- grad_ln2_gain: float32 [1024], replicated
- grad_ln2_bias: float32 [1024], replicated
- grad_qkv_weight: float32 [1024, 3072], P('dp', 'tensor')
- grad_qkv_bias: float32 [3072], P('tensor')
- grad_out_weight: float32 [1024, 1024], P('tensor', 'dp')
- grad_out_bias: float32 [1024], replicated
- grad_up_weight: float32 [1024, 4096], P('dp', 'tensor')
- grad_up_bias: float32 [4096], P('tensor')
- grad_down_weight: float32 [4096, 1024], P('tensor', 'dp')
- grad_down_bias: float32 [1024], replicated
Inputs may be any that keep to these rules, and one draw needn't show every extreme that they name: `seq_lengths`: each row sums to 384, and its longest sequence is exactly 192. `qkv_weight`: A joined projection of fan-in 1024; columns of head h at h * 3 * 64 for queries, keys, then values.
All inputs are finite; a program needn't handle non-finite values.
Results may differ from a plain program's by a relative error of at most 0.0096.
Values may be sent and summed in bfloat16 or wider, within the bound.
No kernel may reach another device: no remote copies, remote signals or barrier semaphores. Data moves between devices by JAX's collectives and lax.ppermute only.
A program may use at most 128 MiB of HBM per device.

v0:
```python
import math

import jax
import jax.numpy as jnp
from jax import lax
from jax.experimental import pallas as pl
from jax.experimental.pallas import tpu as pltpu
from jax.sharding import PartitionSpec as P


HD = 64
ROT = 16


epsilon = 1e-05
masked_score = 1e30
inv_sqrt_two = 0.7071067811865476
inv_sqrt_two_pi = 0.3989422804014327


TN = ((0,), (0,))
NN = ((1,), (0,))
NT = ((1,), (1,))


def sequence_layout(lengths_row, token_ids):
    ends = jnp.cumsum(lengths_row)
    starts = ends - lengths_row
    segment = jnp.sum((token_ids[:, None] >= ends[None, :]).astype(jnp.int32), axis=1)
    member = segment[:, None] == jnp.arange(lengths_row.shape[0], dtype=jnp.int32)[None, :]
    first_token = jnp.sum(jnp.where(member, starts[None, :], 0), axis=1)
    return first_token


def rotary_tables(position, rot_dims):
    half_dims = rot_dims // 2
    freqs = 10000.0 ** (-(jnp.arange(half_dims, dtype=jnp.float32) * 2.0 / rot_dims))
    angles = position.astype(jnp.float32)[:, None] * freqs[None, :]
    cosine = jnp.cos(angles)
    sine = jnp.sin(angles)
    rows = position.shape[0]
    none = jnp.zeros_like(sine)
    ones = jnp.ones((rows, HD - rot_dims), jnp.float32)
    zeros = jnp.zeros((rows, HD - rot_dims), jnp.float32)
    direct = [cosine, cosine, ones]
    later = [-sine, none, zeros]
    earlier = [none, sine, zeros]
    one_head = jnp.ones((rows, HD), jnp.float32)
    no_head = jnp.zeros((rows, HD), jnp.float32)
    return tuple(
        jnp.concatenate(part + part + [last], axis=1)
        for part, last in ((direct, one_head), (later, no_head), (earlier, no_head))
    )


def attention_body(
    first_ref,
    weight_ref,
    bias_ref,
    grad_ref,
    out_ref,
    direct_ref,
    later_ref,
    earlier_ref,
    starts_ref,
    ids_ref,
    keys_ref,
    flat_ref,
    d_joined_ref,
    bias_sum_ref,
    turned_ref,
    d_turned_ref,
):
    heads = weight_ref.shape[1] // (3 * HD)
    half = ROT // 2
    scale = 1.0 / math.sqrt(HD)

    def columns(head, kind):
        start = (3 * head + kind) * HD
        return slice(start, start + HD)

    joined = (
        lax.dot_general(
            first_ref[...], weight_ref[...], (NN, ((), ())), preferred_element_type=jnp.float32
        )
        + bias_ref[...]
    )
    total = joined.shape[1]

    def tiled(ref):
        return jnp.concatenate([ref[...]] * heads, axis=1)

    direct = tiled(direct_ref)
    later = tiled(later_ref)
    earlier = tiled(earlier_ref)
    turned_ref[...] = (
        joined * direct
        + pltpu.roll(joined, total - half, 1) * later
        + pltpu.roll(joined, half, 1) * earlier
    ).astype(jnp.bfloat16)
    d_attended_all = lax.dot_general(
        grad_ref[...], out_ref[...], (NT, ((), ())), preferred_element_type=jnp.float32
    ).astype(jnp.bfloat16)
    allowed = (keys_ref[...] >= starts_ref[...]) & (keys_ref[...] <= ids_ref[...])

    def product(left, right, dims):
        return lax.dot_general(left, right, (dims, ((), ())), preferred_element_type=jnp.float32)

    for head in range(heads):
        query = turned_ref[:, columns(head, 0)]
        key = turned_ref[:, columns(head, 1)]
        value = turned_ref[:, columns(head, 2)]
        d_attended = d_attended_all[:, head * HD : (head + 1) * HD]
        scores = jnp.where(allowed, product(query, key, NT) * scale, -masked_score)
        peak = jnp.max(scores, axis=1, keepdims=True)
        expo = jnp.exp(scores - peak)
        probs = expo / jnp.sum(expo, axis=1, keepdims=True)
        probs_b = probs.astype(jnp.bfloat16)
        attended = product(probs_b, value, NN).astype(jnp.bfloat16)
        flat_ref[:, head * HD : (head + 1) * HD] = attended
        d_probs = product(d_attended, value, NT)
        delta = jnp.sum(
            d_attended.astype(jnp.float32) * attended.astype(jnp.float32), axis=1, keepdims=True
        )
        d_scores = (probs * (d_probs - delta) * scale).astype(jnp.bfloat16)
        d_turned_ref[:, columns(head, 0)] = product(d_scores, key, NN)
        d_turned_ref[:, columns(head, 1)] = product(d_scores, query, TN)
        d_turned_ref[:, columns(head, 2)] = product(probs_b, d_attended, TN)
    d_turned = d_turned_ref[...]
    d_joined = (
        d_turned * direct
        - pltpu.roll(d_turned, total - half, 1) * later
        - pltpu.roll(d_turned, half, 1) * earlier
    )
    bias_sum_ref[...] = jnp.sum(d_joined, axis=0, keepdims=True)
    d_joined_ref[...] = d_joined.astype(jnp.bfloat16)


def attention(first_in, weight, bias, grad_rows, out_weight, tables, first_token, token_ids):
    rows = first_in.shape[0]
    columns = weight.shape[1]
    in_vmem = pl.BlockSpec(memory_space=pltpu.VMEM)
    return pl.pallas_call(
        attention_body,
        in_specs=[in_vmem] * 11,
        out_specs=[in_vmem] * 3,
        out_shape=[
            jax.ShapeDtypeStruct((rows, columns // 3), jnp.bfloat16),
            jax.ShapeDtypeStruct((rows, columns), jnp.bfloat16),
            jax.ShapeDtypeStruct((1, columns), jnp.float32),
        ],
        scratch_shapes=[
            pltpu.VMEM((rows, columns), jnp.bfloat16),
            pltpu.VMEM((rows, columns), jnp.float32),
        ],
        name="attention",
    )(
        first_in,
        weight,
        bias[None, :],
        grad_rows,
        out_weight,
        *tables,
        first_token[:, None],
        token_ids[:, None],
        token_ids[None, :],
    )


def normalize(inputs):
    centered = inputs - jnp.mean(inputs, axis=-1, keepdims=True)
    inv_std = lax.rsqrt(jnp.mean(centered * centered, axis=-1, keepdims=True) + epsilon)
    return (centered * inv_std, inv_std)


def swap(array, axis, bit):
    count = lax.axis_size(axis)
    return lax.ppermute(array, axis, [(i, i ^ (1 << bit)) for i in range(count)])


def axis_bits(axis):
    return lax.axis_size(axis).bit_length() - 1


def relatives(bits):
    found = [0]
    for bit in reversed(bits):
        found = found + [relative | (1 << bit) for relative in found]
    return found


def relative_blocks(array, axis, bits, dim):
    own = lax.axis_index(axis)
    size = array.shape[dim] // lax.axis_size(axis)
    pieces = [
        lax.dynamic_slice_in_dim(array, (own ^ relative) * size, size, dim)
        for relative in relatives(bits)
    ]
    return jnp.concatenate(pieces, axis=dim)


def halves(array, dim):
    middle = array.shape[dim] // 2
    return (
        lax.slice_in_dim(array, 0, middle, axis=dim),
        lax.slice_in_dim(array, middle, 2 * middle, axis=dim),
    )


def fold(keep, send, axis, bits, dim):
    for depth, bit in enumerate(bits):
        arrived = swap(send, axis, bit)
        total = keep + arrived.astype(jnp.float32)
        if depth + 1 < len(bits):
            keep, send = halves(total, dim)
            send = send.astype(jnp.bfloat16)
    return total


def all_sum(array, axis, bits):
    for bit in bits:
        array = array + swap(array, axis, bit)
    return array


def dot(left, right, dims):
    return lax.dot_general(left, right, (dims, ((), ())), preferred_element_type=jnp.float32)


def shards(
    tokens,
    seq_lengths,
    ln1_gain,
    ln1_bias,
    ln2_gain,
    ln2_bias,
    qkv_weight,
    qkv_bias,
    out_weight,
    out_bias,
    up_weight,
    up_bias,
    down_weight,
    down_bias,
    cotangent,
):
    row_count = tokens.shape[0]
    width = tokens.shape[1]
    tensor_bits = list(range(axis_bits("tensor")))
    dp_bits = list(range(axis_bits("dp")))
    y_first = dp_bits
    z_first = dp_bits[1:2] + dp_bits[0:1] + dp_bits[2:]
    own_rank = lax.axis_index("tensor")
    token_ids = jnp.concatenate(
        [
            (own_rank ^ relative) * row_count + jnp.arange(row_count, dtype=jnp.int32)
            for relative in relatives(tensor_bits)
        ]
    )
    first_token = sequence_layout(seq_lengths[0], token_ids)
    tables = rotary_tables(token_ids - first_token, ROT)

    def gather(rows):
        for bit in reversed(tensor_bits):
            rows = jnp.concatenate([rows, swap(rows, "tensor", bit)], axis=0)
        return rows

    whole_rows = gather(tokens)
    grad_rows_all = gather(cotangent)
    whole_normed = normalize(whole_rows.astype(jnp.float32))[0]
    first_in = (whole_normed * ln1_gain + ln1_bias).astype(jnp.bfloat16)
    second_in = (whole_normed * ln2_gain + ln2_bias).astype(jnp.bfloat16)

    first_rel = halves(relative_blocks(first_in, "dp", y_first, 1), 1)
    second_rel = halves(relative_blocks(second_in, "dp", z_first, 1), 1)
    grad_rel = halves(relative_blocks(grad_rows_all, "dp", y_first, 1), 1)

    hidden = dot(second_in, up_weight, NN) + up_bias
    cumulative = 0.5 * (1.0 + lax.erf(hidden * inv_sqrt_two))
    active = (hidden * cumulative).astype(jnp.bfloat16)
    slope = cumulative + hidden * jnp.exp(-0.5 * hidden * hidden) * inv_sqrt_two_pi
    down_send = dot(active, grad_rel[1], TN).astype(jnp.bfloat16)
    down_keep = dot(active, grad_rel[0], TN)
    grad_down_weight = fold(down_keep, down_send, "dp", y_first, 1)

    d_hidden = dot(grad_rows_all, down_weight, NT) * slope
    d_hidden_b = d_hidden.astype(jnp.bfloat16)
    g_up_bias = jnp.sum(d_hidden, axis=0)
    up_send = dot(second_rel[1], d_hidden_b, TN).astype(jnp.bfloat16)
    up_keep = dot(second_rel[0], d_hidden_b, TN)
    grad_up_weight = fold(up_keep, up_send, "dp", z_first, 0)

    flat, d_joined_b, g_qkv_bias = attention(
        first_in,
        qkv_weight,
        qkv_bias,
        grad_rows_all,
        out_weight,
        tables,
        first_token,
        token_ids,
    )
    g_qkv_bias = g_qkv_bias[0]
    qkv_send = dot(first_rel[1], d_joined_b, TN).astype(jnp.bfloat16)
    qkv_keep = dot(first_rel[0], d_joined_b, TN)
    grad_qkv_weight = fold(qkv_keep, qkv_send, "dp", y_first, 0)

    out_send = dot(flat, grad_rel[1], TN).astype(jnp.bfloat16)
    out_keep = dot(flat, grad_rel[0], TN)
    grad_out_weight = fold(out_keep, out_send, "dp", y_first, 1)

    def token_sum(partial):
        keep, send = halves(partial, 0)
        return fold(keep, send.astype(jnp.bfloat16), "tensor", tensor_bits, 0)

    d_first = dot(d_joined_b, qkv_weight, NT)
    d_second = dot(d_hidden_b, up_weight, NT)
    mixed = token_sum(d_first * ln1_gain + d_second * ln2_gain)
    branch = token_sum(dot(flat, out_weight, NN) + dot(active, down_weight, NN))

    norm_sums = jnp.concatenate(
        [
            jnp.sum(d_first * whole_normed, axis=0),
            jnp.sum(d_first, axis=0),
            jnp.sum(d_second * whole_normed, axis=0),
            jnp.sum(d_second, axis=0),
        ]
    )
    norm_sums = all_sum(norm_sums, "tensor", tensor_bits)
    bias_total = jnp.sum(grad_rows_all.astype(jnp.float32), axis=0)
    sums = all_sum(
        jnp.concatenate([norm_sums, bias_total, g_up_bias, g_qkv_bias]), "dp", dp_bits
    )
    gain_one, shift_one, gain_two, shift_two, bias_total = (
        sums[i * width : (i + 1) * width] for i in range(5)
    )
    rest = sums[5 * width :]
    grad_up_bias = rest[: g_up_bias.shape[0]]
    grad_qkv_bias = rest[g_up_bias.shape[0] :]

    rows_float = tokens.astype(jnp.float32)
    normed, inv_std = normalize(rows_float)
    output = (rows_float + branch + out_bias + down_bias).astype(jnp.bfloat16)
    grad_float = cotangent.astype(jnp.float32)
    grad_input = (
        inv_std
        * (
            mixed
            - jnp.mean(mixed, axis=-1, keepdims=True)
            - normed * jnp.mean(mixed * normed, axis=-1, keepdims=True)
        )
        + grad_float
    )
    grad_input = grad_input.astype(jnp.bfloat16)
    return (
        output,
        grad_input,
        gain_one,
        shift_one,
        gain_two,
        shift_two,
        grad_qkv_weight,
        grad_qkv_bias,
        grad_out_weight,
        bias_total,
        grad_up_weight,
        grad_up_bias,
        grad_down_weight,
        bias_total,
    )


def solution(mesh):
    placed = (
        P(("dp", "tensor"), None),
        P("dp", None),
        P(),
        P(),
        P(),
        P(),
        P(None, "tensor"),
        P("tensor"),
        P("tensor", None),
        P(),
        P(None, "tensor"),
        P("tensor"),
        P("tensor", None),
        P(),
        P(("dp", "tensor"), None),
    )
    return jax.shard_map(
        shards,
        mesh=mesh,
        in_specs=placed,
        out_specs=(
            P(("dp", "tensor"), None),
            P(("dp", "tensor"), None),
            P(),
            P(),
            P(),
            P(),
            P("dp", "tensor"),
            P("tensor"),
            P("tensor", "dp"),
            P(),
            P("dp", "tensor"),
            P("tensor"),
            P("tensor", "dp"),
            P(),
        ),
        check_vma=False,
    )
```

profile of v0, /device:TPU:0, one launch (start us, length us, event | category | flops | bytes accessed | tf_op | source)
XLA Modules:
  0.0 156.1 jit_solution(16268022748345886122)
XLA Ops:
  0.7 3.0 %collective-permute-start = (bf16[96,1024]{1,0:T(8,128)(2,1)}, bf16[96,1024]{1,0:T(8,128)(2,1)S(1)}, u32[]{:S(2)}, u32[]{:S(2)}) collective-permute-start(bf16[96,1024]{1,0:T(8,128)(2,1)} %param.15), channel_id=1, source_target_pairs={{0,2},{1,3},{2,0},{3,1},{4,6},{5,7},{6,4},{7,5},{8,10},{9,11},{10,... | collective-permute-start | bytes 589832 | tf_op jit(solution)/shard_map/ppermute | solution.py:178
  14.3 2.1 %concatenate.63.later_ref = f32[384,192]{1,0:T(8,128)} concatenate(f32[384,8]{1,0:T(8,128)} %get-tuple-element.64, f32[384,8]{1,0:T(8,128)S(1)} %broadcast_in_dim.36, f32[384,48]{1,0:T(8,128)S(1)} %broadcast_in_dim.37, f32[384,8]{1,0:T(8,128)} %get-tuple-element.64, f32[384,8]{1,0:T(8,128)S(1)} %broadcast_in_dim.36, f32[384,48]{1,0:T(8,128)S(1)} %broadcast_in_dim.37, ...), dimensions={1} | concatenate | bytes 589824 | tf_op jit(solution)/shard_map/concatenate | solution.py:51
  16.4 2.1 %concatenate.64.earlier_ref = f32[384,192]{1,0:T(8,128)} concatenate(f32[384,8]{1,0:T(8,128)S(1)} %broadcast_in_dim.36, f32[384,8]{1,0:T(8,128)} %get-tuple-element.63, f32[384,48]{1,0:T(8,128)S(1)} %broadcast_in_dim.37, f32[384,8]{1,0:T(8,128)S(1)} %broadcast_in_dim.36, f32[384,8]{1,0:T(8,128)} %get-tuple-element.63, f32[384,48]{1,0:T(8,128)S(1)} %broadcast_in_dim.37, ...), dimensions={1} | concatenate | bytes 589824 | tf_op jit(solution)/shard_map/concatenate | solution.py:51
  23.4 2.1 %multiply_convert_fusion = (bf16[384,1024]{1,0:T(8,128)(2,1)}, f32[384,1024]{1,0:T(8,128)S(1)}) fusion(f32[1024]{0:T(1024)S(1)} %copy-done.52, bf16[384,1024]{1,0:T(8,128)(2,1)S(1)} %get-tuple-element.30, bf16[1024,1024]{1,0:T(8,128)(2,1)S(1)} %copy-done), kind=kOutput, calls=%fused_computation.26 | convolution fusion | flops 807665664 | bytes 5246976 | tf_op jit(solution)/shard_map/dot_general | solution.py:227
  27.0 2.2 %fusion.75 = f32[384,1024]{1,0:T(8,128)} fusion(bf16[1024,1024]{1,0:T(8,128)(2,1)S(1)} %copy-done, bf16[384,1024]{1,0:T(8,128)(2,1)S(1)} %get-tuple-element.69), kind=kOutput, calls=%fused_computation.170 | convolution fusion | flops 805306368 | bytes 4456448 | tf_op jit(solution)/shard_map/dot_general | solution.py:227
  31.5 10.6 %attention.1 = (bf16[384,256]{1,0:T(8,128)(2,1)}, bf16[384,768]{1,0:T(8,128)(2,1)}, f32[1,768]{1,0:T(1,128)}) custom-call(bf16[384,1024]{1,0:T(8,128)(2,1)} %copy-done.4, bf16[1024,768]{1,0:T(8,128)(2,1)} %weight_ref.1, f32[1,768]{1,0:T(1,128)} %broadcast_in_dim.30.bias_ref, bf16[384,1024]{1,0:T(8,128)(2,1)} %copy-done.2, bf16[256,1024]{1,0:T(8,128)(2,1)} %out_ref.1, ...), custom_call_target="tpu_custom_call" | custom-call | tf_op jit(solution)/shard_map/attention/pallas_call | solution.py:143
  42.1 3.3 %fusion.10 = (f32[1024]{0:T(1024)S(1)}, f32[1024]{0:T(1024)S(1)}, f32[1024]{0:T(1024)S(1)}, f32[1024]{0:T(1024)S(1)}, f32[384,1024]{1,0:T(8,128)S(1)}) fusion(f32[384]{0:T(512)S(1)} %add_rsqrt_fusion, f32[384]{0:T(512)S(1)} %broadcast_multiply_fusion, bf16[192,1024]{1,0:T(8,128)(2,1)S(1)} %collective-permute-done.1, bf16[96,1024]{1,0:T(8,128)(2,1)S(1)} %copy-done.7, ...), kind=kOutput, calls=%fused_computation.15 | convolution fusion | flops 610660352 | bytes 6122496 | tf_op jit(solution)/shard_map/dot_general | solution.py:227
  46.3 2.2 %fusion.81 = f32[384,1024]{1,0:T(8,128)} fusion(bf16[384,1024]{1,0:T(8,128)(2,1)S(1)} %copy-done.12, bf16[1024,1024]{1,0:T(8,128)(2,1)S(1)} %copy-done.48), kind=kOutput, calls=%fused_computation.176 | convolution fusion | flops 805306368 | bytes 4456448 | tf_op jit(solution)/shard_map/dot_general | solution.py:227
  51.8 2.1 %collective-permute-start.9 = (f32[4096]{0:T(1024)S(1)}, f32[4096]{0:T(1024)S(1)}, u32[]{:S(2)}, u32[]{:S(2)}) collective-permute-start(f32[4096]{0:T(1024)S(1)} %fusion.77), channel_id=1, source_target_pairs={{0,2},{1,3},{2,0},{3,1},{4,6},{5,7},{6,4},{7,5},{8,10},{9,11},{10,... | collective-permute-start | bytes 49160 | tf_op jit(solution)/shard_map/ppermute | solution.py:178
  55.7 2.1 %collective-permute-start.10 = (f32[6912]{0:T(1024)S(1)}, f32[6912]{0:T(1024)S(1)}, u32[]{:S(2)}, u32[]{:S(2)}) collective-permute-start(f32[6912]{0:T(1024)S(1)} %pad_maximum_fusion.9), channel_id=1, source_target_pairs={{0,4},{4,0},{8,12},{12,8},{16,20},{20,16},{24,28},{28,24},{1,5},{5... | collective-permute-start | bytes 82952 | tf_op jit(solution)/shard_map/ppermute | solution.py:178
  57.8 1.9 %convolution_add_fusion.1 = f32[384,1024]{1,0:T(8,128)S(1)} fusion(f32[384,1024]{1,0:T(8,128)} %fusion.81, bf16[384,256]{1,0:T(8,128)(2,1)} %get-tuple-element.17, bf16[256,1024]{1,0:T(8,128)(2,1)S(1)} %copy-done.8), kind=kOutput, calls=%fused_computation.31 | convolution fusion | flops 201719808 | bytes 3866624 | tf_op jit(solution)/shard_map/dot_general | solution.py:227
  59.9 1.8 %collective-permute-start.11 = (f32[6912]{0:T(1024)S(1)}, f32[6912]{0:T(1024)S(1)}, u32[]{:S(2)}, u32[]{:S(2)}) collective-permute-start(f32[6912]{0:T(1024)S(1)} %fusion.78), channel_id=1, source_target_pairs={{0,8},{4,12},{8,0},{12,4},{16,24},{20,28},{24,16},{28,20},{1,9},{5... | collective-permute-start | bytes 82952 | tf_op jit(solution)/shard_map/ppermute | solution.py:178
  64.4 2.7 %collective-permute-start.12 = (f32[6912]{0:T(1024)S(1)}, f32[6912]{0:T(1024)S(1)}, u32[]{:S(2)}, u32[]{:S(2)}) collective-permute-start(f32[6912]{0:T(1024)S(1)} %add.254), channel_id=1, source_target_pairs={{0,16},{4,20},{8,24},{12,28},{16,0},{20,4},{24,8},{28,12},{1,17},{... | collective-permute-start | bytes 82952 | tf_op jit(solution)/shard_map/ppermute | solution.py:178
  70.9 16.6 %collective-permute-done.16 = bf16[256,512]{1,0:T(8,128)(2,1)S(1)} collective-permute-done((bf16[256,512]{1,0:T(8,128)(2,1)S(1)}, bf16[256,512]{1,0:T(8,128)(2,1)S(1)}, u32[]{:S(2)}, u32[]{:S(2)}) %collective-permute-start.16) | collective-permute-done | bytes 262176 | tf_op jit(solution)/shard_map/ppermute | solution.py:178
  89.0 6.8 %collective-permute-done.17 = bf16[256,256]{1,0:T(8,128)(2,1)S(1)} collective-permute-done((bf16[256,256]{1,0:T(8,128)(2,1)S(1)}, bf16[256,256]{1,0:T(8,128)(2,1)S(1)}, u32[]{:S(2)}, u32[]{:S(2)}) %collective-permute-start.17) | collective-permute-done | bytes 131104 | tf_op jit(solution)/shard_map/ppermute | solution.py:178
  96.4 2.5 %collective-permute-start.18 = (bf16[256,128]{1,0:T(8,128)(2,1)S(1)}, bf16[256,128]{1,0:T(8,128)(2,1)S(1)}, u32[]{:S(2)}, u32[]{:S(2)}) collective-permute-start(bf16[256,128]{1,0:T(8,128)(2,1)S(1)} %slice.225), channel_id=1, source_target_pairs={{0,16},{4,20},{8,24},{12,28},{16,0},{20,4},{24,8},{28,12},{1,17},{... | collective-permute-start | bytes 196616 | tf_op jit(solution)/shard_map/ppermute | solution.py:178
  106.0 1.9 %collective-permute-done.5 = bf16[96,1024]{1,0:T(8,128)(2,1)S(1)} collective-permute-done((bf16[96,1024]{1,0:T(8,128)(2,1)S(1)}, bf16[96,1024]{1,0:T(8,128)(2,1)S(1)}, u32[]{:S(2)}, u32[]{:S(2)}) %collective-permute-start.5) | collective-permute-done | bytes 196640 | tf_op jit(solution)/shard_map/ppermute | solution.py:178
  112.6 9.2 %collective-permute-done.22 = bf16[1024,512]{1,0:T(8,128)(2,1)S(1)} collective-permute-done((bf16[1024,512]{1,0:T(8,128)(2,1)S(1)}, bf16[1024,512]{1,0:T(8,128)(2,1)S(1)}, u32[]{:S(2)}, u32[]{:S(2)}) %collective-permute-start.22) | collective-permute-done | bytes 1048608 | tf_op jit(solution)/shard_map/ppermute | solution.py:178
  123.4 2.6 %collective-permute-start.15 = (bf16[128,768]{1,0:T(8,128)(2,1)S(1)}, bf16[128,768]{1,0:T(8,128)(2,1)S(1)}, u32[]{:S(2)}, u32[]{:S(2)}) collective-permute-start(bf16[128,768]{1,0:T(8,128)(2,1)S(1)} %slice.221), channel_id=1, source_target_pairs={{0,16},{4,20},{8,24},{12,28},{16,0},{20,4},{24,8},{28,12},{1,17},{... | collective-permute-start | bytes 589832 | tf_op jit(solution)/shard_map/ppermute | solution.py:178
  125.9 3.9 %collective-permute-done.20 = bf16[256,1024]{1,0:T(8,128)(2,1)S(1)} collective-permute-done((bf16[256,1024]{1,0:T(8,128)(2,1)S(1)}, bf16[256,1024]{1,0:T(8,128)(2,1)S(1)}, u32[]{:S(2)}, u32[]{:S(2)}) %collective-permute-start.20) | collective-permute-done | bytes 524320 | tf_op jit(solution)/shard_map/ppermute | solution.py:178
  130.1 2.0 %collective-permute-start.21 = (bf16[128,1024]{1,0:T(8,128)(2,1)S(1)}, bf16[128,1024]{1,0:T(8,128)(2,1)S(1)}, u32[]{:S(2)}, u32[]{:S(2)}) collective-permute-start(bf16[128,1024]{1,0:T(8,128)(2,1)S(1)} %slice.220), channel_id=1, source_target_pairs={{0,16},{4,20},{8,24},{12,28},{16,0},{20,4},{24,8},{28,12},{1,17},{... | collective-permute-start | bytes 786440 | tf_op jit(solution)/shard_map/ppermute | solution.py:178
  132.1 6.3 %collective-permute-done.23 = bf16[1024,256]{1,0:T(8,128)(2,1)S(1)} collective-permute-done((bf16[1024,256]{1,0:T(8,128)(2,1)S(1)}, bf16[1024,256]{1,0:T(8,128)(2,1)S(1)}, u32[]{:S(2)}, u32[]{:S(2)}) %collective-permute-start.23) | collective-permute-done | bytes 524320 | tf_op jit(solution)/shard_map/ppermute | solution.py:178
  140.7 10.3 %collective-permute-done.21 = bf16[128,1024]{1,0:T(8,128)(2,1)S(1)} collective-permute-done((bf16[128,1024]{1,0:T(8,128)(2,1)S(1)}, bf16[128,1024]{1,0:T(8,128)(2,1)S(1)}, u32[]{:S(2)}, u32[]{:S(2)}) %collective-permute-start.21) | collective-permute-done | bytes 262176 | tf_op jit(solution)/shard_map/ppermute | solution.py:178
  151.9 2.7 %collective-permute-done.24 = bf16[1024,128]{1,0:T(8,128)(2,1)S(1)} collective-permute-done((bf16[1024,128]{1,0:T(8,128)(2,1)S(1)}, bf16[1024,128]{1,0:T(8,128)(2,1)S(1)}, u32[]{:S(2)}, u32[]{:S(2)}) %collective-permute-start.24) | collective-permute-done | bytes 262176 | tf_op jit(solution)/shard_map/ppermute | solution.py:178
  (223 shorter events, 51.6 us)
Async XLA Ops:
  0.7 9.0 %collective-permute-start = (bf16[96,1024]{1,0:T(8,128)(2,1)}, bf16[96,1024]{1,0:T(8,128)(2,1)S(1)}, u32[]{:S(2)}, u32[]{:S(2)}) collective-permute-start(bf16[96,1024]{1,0:T(8,128)(2,1)} %param.15), channel_id=1, source_target_pairs={{0,2},{1,3},{2,0},{3,1},{4,6},{5,7},{6,4},{7,5},{8,10},{9,11},{10,... | collective-permute-start | bytes 589832 | tf_op jit(solution)/shard_map/ppermute | solution.py:178
  3.7 16.0 %collective-permute-start.2 = (bf16[96,1024]{1,0:T(8,128)(2,1)}, bf16[96,1024]{1,0:T(8,128)(2,1)}, u32[]{:S(2)}, u32[]{:S(2)}) collective-permute-start(bf16[96,1024]{1,0:T(8,128)(2,1)} %param.29), channel_id=1, source_target_pairs={{0,2},{1,3},{2,0},{3,1},{4,6},{5,7},{6,4},{7,5},{8,10},{9,11},{10,... | collective-permute-start | bytes 589832 | tf_op jit(solution)/shard_map/ppermute | solution.py:178
  11.4 10.8 %collective-permute-start.1 = (bf16[192,1024]{1,0:T(8,128)(2,1)}, bf16[192,1024]{1,0:T(8,128)(2,1)S(1)}, u32[]{:S(2)}, u32[]{:S(2)}) collective-permute-start(bf16[192,1024]{1,0:T(8,128)(2,1)} %pad_maximum_fusion.1), channel_id=1, source_target_pairs={{0,1},{1,0},{2,3},{3,2},{4,5},{5,4},{6,7},{7,6},{8,9},{9,8},{10,11... | collective-permute-start | bytes 1179656 | tf_op jit(solution)/shard_map/ppermute | solution.py:178
  20.7 4.8 %collective-permute-start.3 = (bf16[192,1024]{1,0:T(8,128)(2,1)S(1)}, bf16[192,1024]{1,0:T(8,128)(2,1)S(1)}, u32[]{:S(2)}, u32[]{:S(2)}) collective-permute-start(bf16[192,1024]{1,0:T(8,128)(2,1)S(1)} %pad_maximum_fusion.2), channel_id=1, source_target_pairs={{0,1},{1,0},{2,3},{3,2},{4,5},{5,4},{6,7},{7,6},{8,9},{9,8},{10,11... | collective-permute-start | bytes 1179656 | tf_op jit(solution)/shard_map/ppermute | solution.py:178
  46.2 50.1 %collective-permute-start.6 = (bf16[192,1024]{1,0:T(8,128)(2,1)}, bf16[192,1024]{1,0:T(8,128)(2,1)}, u32[]{:S(2)}, u32[]{:S(2)}) collective-permute-start(bf16[192,1024]{1,0:T(8,128)(2,1)} %slice.217), channel_id=1, source_target_pairs={{0,1},{1,0},{2,3},{3,2},{4,5},{5,4},{6,7},{7,6},{8,9},{9,8},{10,11... | collective-permute-start | bytes 1179656 | tf_op jit(solution)/shard_map/ppermute | solution.py:178
  51.8 3.8 %collective-permute-start.9 = (f32[4096]{0:T(1024)S(1)}, f32[4096]{0:T(1024)S(1)}, u32[]{:S(2)}, u32[]{:S(2)}) collective-permute-start(f32[4096]{0:T(1024)S(1)} %fusion.77), channel_id=1, source_target_pairs={{0,2},{1,3},{2,0},{3,1},{4,6},{5,7},{6,4},{7,5},{8,10},{9,11},{10,... | collective-permute-start | bytes 49160 | tf_op jit(solution)/shard_map/ppermute | solution.py:178
  55.7 4.2 %collective-permute-start.10 = (f32[6912]{0:T(1024)S(1)}, f32[6912]{0:T(1024)S(1)}, u32[]{:S(2)}, u32[]{:S(2)}) collective-permute-start(f32[6912]{0:T(1024)S(1)} %pad_maximum_fusion.9), channel_id=1, source_target_pairs={{0,4},{4,0},{8,12},{12,8},{16,20},{20,16},{24,28},{28,24},{1,5},{5... | collective-permute-start | bytes 82952 | tf_op jit(solution)/shard_map/ppermute | solution.py:178
  59.8 40.3 %collective-permute-start.4 = (bf16[192,1024]{1,0:T(8,128)(2,1)S(1)}, bf16[192,1024]{1,0:T(8,128)(2,1)S(1)}, u32[]{:S(2)}, u32[]{:S(2)}) collective-permute-start(bf16[192,1024]{1,0:T(8,128)(2,1)S(1)} %slice.218), channel_id=1, source_target_pairs={{0,1},{1,0},{2,3},{3,2},{4,5},{5,4},{6,7},{7,6},{8,9},{9,8},{10,11... | collective-permute-start | bytes 1179656 | tf_op jit(solution)/shard_map/ppermute | solution.py:178
  59.9 4.5 %collective-permute-start.11 = (f32[6912]{0:T(1024)S(1)}, f32[6912]{0:T(1024)S(1)}, u32[]{:S(2)}, u32[]{:S(2)}) collective-permute-start(f32[6912]{0:T(1024)S(1)} %fusion.78), channel_id=1, source_target_pairs={{0,8},{4,12},{8,0},{12,4},{16,24},{20,28},{24,16},{28,20},{1,9},{5... | collective-permute-start | bytes 82952 | tf_op jit(solution)/shard_map/ppermute | solution.py:178
  62.3 46.6 %collective-permute-start.13 = (bf16[512,768]{1,0:T(8,128)(2,1)S(1)}, bf16[512,768]{1,0:T(8,128)(2,1)S(1)}, u32[]{:S(2)}, u32[]{:S(2)}) collective-permute-start(bf16[512,768]{1,0:T(8,128)(2,1)S(1)} %convolution_convert_fusion.2), channel_id=1, source_target_pairs={{0,4},{4,0},{8,12},{12,8},{16,20},{20,16},{24,28},{28,24},{1,5},{5... | collective-permute-start | bytes 2359304 | tf_op jit(solution)/shard_map/ppermute | solution.py:178
  63.9 23.6 %collective-permute-start.16 = (bf16[256,512]{1,0:T(8,128)(2,1)S(1)}, bf16[256,512]{1,0:T(8,128)(2,1)S(1)}, u32[]{:S(2)}, u32[]{:S(2)}) collective-permute-start(bf16[256,512]{1,0:T(8,128)(2,1)S(1)} %copy-done.51), channel_id=1, source_target_pairs={{0,4},{4,0},{8,12},{12,8},{16,20},{20,16},{24,28},{28,24},{1,5},{5... | collective-permute-start | bytes 786440 | tf_op jit(solution)/shard_map/ppermute | solution.py:178
  64.4 4.8 %collective-permute-start.12 = (f32[6912]{0:T(1024)S(1)}, f32[6912]{0:T(1024)S(1)}, u32[]{:S(2)}, u32[]{:S(2)}) collective-permute-start(f32[6912]{0:T(1024)S(1)} %add.254), channel_id=1, source_target_pairs={{0,16},{4,20},{8,24},{12,28},{16,0},{20,4},{24,8},{28,12},{1,17},{... | collective-permute-start | bytes 82952 | tf_op jit(solution)/shard_map/ppermute | solution.py:178
  69.3 41.3 %collective-permute-start.19 = (bf16[512,1024]{1,0:T(8,128)(2,1)S(1)}, bf16[512,1024]{1,0:T(8,128)(2,1)S(1)}, u32[]{:S(2)}, u32[]{:S(2)}) collective-permute-start(bf16[512,1024]{1,0:T(8,128)(2,1)S(1)} %convolution_convert_fusion.1), channel_id=1, source_target_pairs={{0,8},{4,12},{8,0},{12,4},{16,24},{20,28},{24,16},{28,20},{1,9},{5... | collective-permute-start | bytes 3145736 | tf_op jit(solution)/shard_map/ppermute | solution.py:178
  87.9 7.9 %collective-permute-start.17 = (bf16[256,256]{1,0:T(8,128)(2,1)S(1)}, bf16[256,256]{1,0:T(8,128)(2,1)S(1)}, u32[]{:S(2)}, u32[]{:S(2)}) collective-permute-start(bf16[256,256]{1,0:T(8,128)(2,1)S(1)} %slice.224), channel_id=1, source_target_pairs={{0,8},{4,12},{8,0},{12,4},{16,24},{20,28},{24,16},{28,20},{1,9},{5... | collective-permute-start | bytes 393224 | tf_op jit(solution)/shard_map/ppermute | solution.py:178
  95.8 26.0 %collective-permute-start.22 = (bf16[1024,512]{1,0:T(8,128)(2,1)S(1)}, bf16[1024,512]{1,0:T(8,128)(2,1)S(1)}, u32[]{:S(2)}, u32[]{:S(2)}) collective-permute-start(bf16[1024,512]{1,0:T(8,128)(2,1)S(1)} %copy-done.49), channel_id=1, source_target_pairs={{0,4},{4,0},{8,12},{12,8},{16,20},{20,16},{24,28},{28,24},{1,5},{5... | collective-permute-start | bytes 3145736 | tf_op jit(solution)/shard_map/ppermute | solution.py:178
  96.4 5.9 %collective-permute-start.18 = (bf16[256,128]{1,0:T(8,128)(2,1)S(1)}, bf16[256,128]{1,0:T(8,128)(2,1)S(1)}, u32[]{:S(2)}, u32[]{:S(2)}) collective-permute-start(bf16[256,128]{1,0:T(8,128)(2,1)S(1)} %slice.225), channel_id=1, source_target_pairs={{0,16},{4,20},{8,24},{12,28},{16,0},{20,4},{24,8},{28,12},{1,17},{... | collective-permute-start | bytes 196616 | tf_op jit(solution)/shard_map/ppermute | solution.py:178
  100.1 5.7 %collective-permute-start.7 = (bf16[96,1024]{1,0:T(8,128)(2,1)S(1)}, bf16[96,1024]{1,0:T(8,128)(2,1)S(1)}, u32[]{:S(2)}, u32[]{:S(2)}) collective-permute-start(bf16[96,1024]{1,0:T(8,128)(2,1)S(1)} %slice.222), channel_id=1, source_target_pairs={{0,2},{1,3},{2,0},{3,1},{4,6},{5,7},{6,4},{7,5},{8,10},{9,11},{10,... | collective-permute-start | bytes 589832 | tf_op jit(solution)/shard_map/ppermute | solution.py:178
  102.3 5.7 %collective-permute-start.5 = (bf16[96,1024]{1,0:T(8,128)(2,1)S(1)}, bf16[96,1024]{1,0:T(8,128)(2,1)S(1)}, u32[]{:S(2)}, u32[]{:S(2)}) collective-permute-start(bf16[96,1024]{1,0:T(8,128)(2,1)S(1)} %slice.223), channel_id=1, source_target_pairs={{0,2},{1,3},{2,0},{3,1},{4,6},{5,7},{6,4},{7,5},{8,10},{9,11},{10,... | collective-permute-start | bytes 589832 | tf_op jit(solution)/shard_map/ppermute | solution.py:178
  109.6 13.6 %collective-permute-start.14 = (bf16[256,768]{1,0:T(8,128)(2,1)S(1)}, bf16[256,768]{1,0:T(8,128)(2,1)S(1)}, u32[]{:S(2)}, u32[]{:S(2)}) collective-permute-start(bf16[256,768]{1,0:T(8,128)(2,1)S(1)} %slice.216), channel_id=1, source_target_pairs={{0,8},{4,12},{8,0},{12,4},{16,24},{20,28},{24,16},{28,20},{1,9},{5... | collective-permute-start | bytes 1179656 | tf_op jit(solution)/shard_map/ppermute | solution.py:178
  111.3 18.5 %collective-permute-start.20 = (bf16[256,1024]{1,0:T(8,128)(2,1)S(1)}, bf16[256,1024]{1,0:T(8,128)(2,1)S(1)}, u32[]{:S(2)}, u32[]{:S(2)}) collective-permute-start(bf16[256,1024]{1,0:T(8,128)(2,1)S(1)} %slice.215), channel_id=1, source_target_pairs={{0,4},{4,0},{8,12},{12,8},{16,20},{20,16},{24,28},{28,24},{1,5},{5... | collective-permute-start | bytes 1572872 | tf_op jit(solution)/shard_map/ppermute | solution.py:178
  122.6 15.8 %collective-permute-start.23 = (bf16[1024,256]{1,0:T(8,128)(2,1)S(1)}, bf16[1024,256]{1,0:T(8,128)(2,1)S(1)}, u32[]{:S(2)}, u32[]{:S(2)}) collective-permute-start(bf16[1024,256]{1,0:T(8,128)(2,1)S(1)} %slice.214), channel_id=1, source_target_pairs={{0,8},{4,12},{8,0},{12,4},{16,24},{20,28},{24,16},{28,20},{1,9},{5... | collective-permute-start | bytes 1572872 | tf_op jit(solution)/shard_map/ppermute | solution.py:178
  123.4 16.5 %collective-permute-start.15 = (bf16[128,768]{1,0:T(8,128)(2,1)S(1)}, bf16[128,768]{1,0:T(8,128)(2,1)S(1)}, u32[]{:S(2)}, u32[]{:S(2)}) collective-permute-start(bf16[128,768]{1,0:T(8,128)(2,1)S(1)} %slice.221), channel_id=1, source_target_pairs={{0,16},{4,20},{8,24},{12,28},{16,0},{20,4},{24,8},{28,12},{1,17},{... | collective-permute-start | bytes 589832 | tf_op jit(solution)/shard_map/ppermute | solution.py:178
  130.1 21.0 %collective-permute-start.21 = (bf16[128,1024]{1,0:T(8,128)(2,1)S(1)}, bf16[128,1024]{1,0:T(8,128)(2,1)S(1)}, u32[]{:S(2)}, u32[]{:S(2)}) collective-permute-start(bf16[128,1024]{1,0:T(8,128)(2,1)S(1)} %slice.220), channel_id=1, source_target_pairs={{0,16},{4,20},{8,24},{12,28},{16,0},{20,4},{24,8},{28,12},{1,17},{... | collective-permute-start | bytes 786440 | tf_op jit(solution)/shard_map/ppermute | solution.py:178
  138.6 16.0 %collective-permute-start.24 = (bf16[1024,128]{1,0:T(8,128)(2,1)S(1)}, bf16[1024,128]{1,0:T(8,128)(2,1)S(1)}, u32[]{:S(2)}, u32[]{:S(2)}) collective-permute-start(bf16[1024,128]{1,0:T(8,128)(2,1)S(1)} %slice.219), channel_id=1, source_target_pairs={{0,16},{4,20},{8,24},{12,28},{16,0},{20,4},{24,8},{28,12},{1,17},{... | collective-permute-start | bytes 786440 | tf_op jit(solution)/shard_map/ppermute | solution.py:178
  (54 other events, 481.9 us)
where the time goes:
time: 156 us
  waiting for transfers between devices  62.9 us (40%)
  starting transfers between devices  31.3 us (20%)
  matrix products  19.6 us (13%)
  other arithmetic  15.6 us (10%)
  local copies, waits for them, and re-layouts  14.7 us (9%)
  Pallas kernels  10.6 us (7%)
    ppermute x25, waiting for transfers between devices, swap(): return lax.ppermute(array, axis, [(i, i ^ 1 << bit) for i in range(count)])  62.9 us
    ppermute x25, starting transfers between devices, swap(): return lax.ppermute(array, axis, [(i, i ^ 1 << bit) for i in range(count)])  31.3 us
    dot_general x14, matrix products, dot(): lax.dot_general(left, right, (dims, ((), ())), preferred_element_type=jnp...  19.6 us
    pallas_call x1, Pallas kernels, attention(): pl.pallas_call(attention_body, in_specs=[in_vmem] * 11, out_specs=[in_vme...  10.6 us
    concatenate x3, local copies, waits for them, and re-layouts, rotary_tables(): jnp.concatenate(part + part + [last], axis=1)  5.31 us
    add x10, other arithmetic, fold(): total = keep + arrived.astype(jnp.float32)  4.74 us
  transfers between devices with their start and end apart: 25, of which 13 were waited for; matrix products, arithmetic and copies ran while one was open for 24% of the time, Pallas kernels for 0%

commit v1 on v0

v1 whole, which is shorter than its diff:
```python
import math

import jax
import jax.numpy as jnp
from jax import lax
from jax.experimental import pallas as pl
from jax.experimental.pallas import tpu as pltpu
from jax.sharding import PartitionSpec as P


HD = 64
ROT = 16


epsilon = 1e-05
masked_score = 1e30
inv_sqrt_two = 0.7071067811865476
inv_sqrt_two_pi = 0.3989422804014327


TN = ((0,), (0,))
NN = ((1,), (0,))
NT = ((1,), (1,))


def token_places(ids_ref, axis, shape):
    blocks = ids_ref.shape[0]
    size = shape[axis] // blocks
    place = lax.broadcasted_iota(jnp.int32, shape, axis)
    found = place + ids_ref[0]
    for block in range(1, blocks):
        shift = ids_ref[block] - block * size
        found = jnp.where(place >= block * size, place + shift, found)
    return found


def rotary_and_mask(ids_ref, lengths_ref, rows):
    columns = 2 * HD
    half = ROT // 2
    ids = token_places(ids_ref, 0, (rows, columns))
    first_token = jnp.zeros_like(ids)
    start = jnp.int32(0)
    for index in range(lengths_ref.shape[1]):
        first_token = jnp.where(ids >= start, start, first_token)
        start = start + lengths_ref[0, index]
    position = (ids - first_token).astype(jnp.float32)
    lane = lax.broadcasted_iota(jnp.int32, (1, columns), 1)
    within = lane % HD
    power = (within % half).astype(jnp.float32) * (-2.0 / ROT * math.log(10000.0))
    angles = position * jnp.where(within < ROT, jnp.exp(power), 0.0)
    cosine = jnp.cos(angles)
    sine = jnp.sin(angles)
    left = lane < HD

    def spread(pattern, rest):
        return jnp.concatenate(
            [pattern, jnp.where(left, rest, pattern), jnp.where(left, pattern, rest)], axis=1
        )

    direct = spread(cosine, 1.0)
    later = spread(jnp.where(within < half, -sine, 0.0), 0.0)
    earlier = spread(jnp.where(within < half, 0.0, sine), 0.0)
    keys = token_places(ids_ref, 1, (1, rows))
    allowed = (keys >= first_token[:, :1]) & (keys <= ids[:, :1])
    return direct, later, earlier, jnp.where(allowed, 0.0, -masked_score)


def pack_body(affine_ref, weight_ref, target_ref):
    del weight_ref
    target_ref[...] = affine_ref[...]


def pack(affine, weight):
    in_vmem = pl.BlockSpec(memory_space=pltpu.VMEM)
    return pl.pallas_call(
        pack_body,
        in_specs=[in_vmem] * 2,
        out_specs=in_vmem,
        out_shape=jax.ShapeDtypeStruct(affine.shape, affine.dtype),
        compiler_params=pltpu.CompilerParams(vmem_limit_bytes=4 << 20),
        name="pack",
    )(affine, weight)


def copy_relative(places_ref, start, target_ref, source_ref):
    size = 128
    count = target_ref.shape[1] // size
    for place in range(count):
        origin = pl.multiple_of(places_ref[start + place] * size, size)
        target_ref[:, place * size : (place + 1) * size] = source_ref[:, pl.ds(origin, size)]


def fetch(row_refs, target_ref, arrival):
    size = row_refs[0].shape[0]
    copies = [
        pltpu.make_async_copy(
            row_ref, target_ref.at[pl.ds(index * size, size), :], arrival.at[index]
        )
        for index, row_ref in enumerate(row_refs)
    ]
    for copy in copies:
        copy.start()
    return copies


def piece_specs(pieces):
    own = pl.BlockSpec(memory_space=pltpu.HBM)
    return [own] + [pl.BlockSpec(memory_space=pl.ANY)] * (len(pieces) - 1)


def front_body(*refs, blocks, relative):
    refs = list(refs)
    places_ref = refs.pop(0)
    row_refs = [refs.pop(0) for _ in range(blocks)]
    affine_ref, weight_ref, second_ref, active_ref, slope_ref = (refs.pop(0) for _ in range(5))
    arrival, rows_ref = refs.pop(-1), refs.pop(-1)
    size = row_refs[0].shape[0]
    for index, copy in enumerate(fetch(row_refs, rows_ref, arrival)):
        copy.wait()
        rows = slice(index * size, (index + 1) * size)
        normed, _ = normalize(rows_ref[rows, :].astype(jnp.float32))
        second_ref[rows, :] = (normed * affine_ref[2:3, :] + affine_ref[3:4, :]).astype(
            jnp.bfloat16
        )
    if relative:
        copy_relative(places_ref, second_ref.shape[1] // 128, refs[0], second_ref)
    hidden = (
        lax.dot_general(
            second_ref[...], weight_ref[...], (NN, ((), ())), preferred_element_type=jnp.float32
        )
        + jnp.concatenate(
            [affine_ref[row : row + 1, :] for row in range(4, affine_ref.shape[0])], axis=1
        )
    )
    cumulative = 0.5 * (1.0 + lax.erf(hidden * inv_sqrt_two))
    active_ref[...] = (hidden * cumulative).astype(jnp.bfloat16)
    slope_ref[...] = cumulative + hidden * jnp.exp(-0.5 * hidden * hidden) * inv_sqrt_two_pi


def front(places, pieces, affine, weight, relative):
    size, width = pieces[0].shape
    rows = size * len(pieces)
    units = weight.shape[1]
    in_smem = pl.BlockSpec(memory_space=pltpu.SMEM)
    in_vmem = pl.BlockSpec(memory_space=pltpu.VMEM)
    narrow = jax.ShapeDtypeStruct((rows, width), jnp.bfloat16)
    shapes = [
        narrow,
        jax.ShapeDtypeStruct((rows, units), jnp.bfloat16),
        jax.ShapeDtypeStruct((rows, units), jnp.float32),
    ]
    shapes += [narrow] if relative else []
    return pl.pallas_call(
        lambda *refs: front_body(*refs, blocks=len(pieces), relative=relative),
        in_specs=[in_smem] + piece_specs(pieces) + [in_vmem] * 2,
        out_specs=[in_vmem] * len(shapes),
        out_shape=shapes,
        scratch_shapes=[
            pltpu.VMEM((rows, width), jnp.bfloat16),
            pltpu.SemaphoreType.DMA((len(pieces),)),
        ],
        compiler_params=pltpu.CompilerParams(vmem_limit_bytes=14 << 20),
        name="front",
    )(places, *pieces, affine, weight)


def join_body(*refs, blocks, relative):
    refs = list(refs)
    places_ref = refs.pop(0)
    row_refs = [refs.pop(0) for _ in range(blocks)]
    arrival = refs.pop(-1)
    whole_ref = refs.pop(0)
    for copy in fetch(row_refs, whole_ref, arrival):
        copy.wait()
    if relative:
        copy_relative(places_ref, 0, refs[0], whole_ref)


def join(places, pieces, relative):
    size, width = pieces[0].shape
    rows = size * len(pieces)
    in_smem = pl.BlockSpec(memory_space=pltpu.SMEM)
    in_vmem = pl.BlockSpec(memory_space=pltpu.VMEM)
    shapes = [jax.ShapeDtypeStruct((rows, width), jnp.bfloat16)] * (2 if relative else 1)
    return pl.pallas_call(
        lambda *refs: join_body(*refs, blocks=len(pieces), relative=relative),
        in_specs=[in_smem] + piece_specs(pieces),
        out_specs=[in_vmem] * len(shapes),
        out_shape=shapes,
        scratch_shapes=[pltpu.SemaphoreType.DMA((len(pieces),))],
        compiler_params=pltpu.CompilerParams(vmem_limit_bytes=8 << 20),
        name="join",
    )(places, *pieces)


def norm_body(*refs, blocks, relative):
    refs = list(refs)
    places_ref = refs.pop(0)
    row_refs = [refs.pop(0) for _ in range(blocks)]
    affine_ref, grad_ref = (refs.pop(0) for _ in range(2))
    first_ref, normed_ref, scale_ref, sum_ref = (refs.pop(0) for _ in range(4))
    arrival, rows_ref = refs.pop(-1), refs.pop(-1)
    size = row_refs[0].shape[0]
    for index, copy in enumerate(fetch(row_refs, rows_ref, arrival)):
        copy.wait()
        rows = slice(index * size, (index + 1) * size)
        normed, inv_std = normalize(rows_ref[rows, :].astype(jnp.float32))
        normed_ref[rows, :] = normed
        first_ref[rows, :] = (normed * affine_ref[0:1, :] + affine_ref[1:2, :]).astype(jnp.bfloat16)
        if index == 0:
            scale_ref[...] = inv_std
    sum_ref[...] = jnp.sum(grad_ref[...].astype(jnp.float32), axis=0, keepdims=True)
    if relative:
        count = first_ref.shape[1] // 128
        copy_relative(places_ref, 0, refs[0], first_ref)
        copy_relative(places_ref, count, refs[1], grad_ref)


def norm(places, pieces, affine, grad_rows, relative):
    size, width = pieces[0].shape
    rows = size * len(pieces)
    in_smem = pl.BlockSpec(memory_space=pltpu.SMEM)
    in_vmem = pl.BlockSpec(memory_space=pltpu.VMEM)
    narrow = jax.ShapeDtypeStruct((rows, width), jnp.bfloat16)
    shapes = [
        narrow,
        jax.ShapeDtypeStruct((rows, width), jnp.float32),
        jax.ShapeDtypeStruct((size, 1), jnp.float32),
        jax.ShapeDtypeStruct((1, width), jnp.float32),
    ]
    shapes += [narrow] * 2 if relative else []
    return pl.pallas_call(
        lambda *refs: norm_body(*refs, blocks=len(pieces), relative=relative),
        in_specs=[in_smem] + piece_specs(pieces) + [in_vmem] * 2,
        out_specs=[in_vmem] * len(shapes),
        out_shape=shapes,
        scratch_shapes=[
            pltpu.VMEM((rows, width), jnp.bfloat16),
            pltpu.SemaphoreType.DMA((len(pieces),)),
        ],
        compiler_params=pltpu.CompilerParams(vmem_limit_bytes=8 << 20),
        name="norm",
    )(places, *pieces, affine, grad_rows)


def mix_body(
    d_joined_ref,
    qkv_ref,
    d_hidden_ref,
    up_ref,
    normed_ref,
    affine_ref,
    flat_ref,
    out_ref,
    active_ref,
    down_ref,
    keep_ref,
    send_ref,
    sums_ref,
):
    def product(left_ref, right_ref, dims):
        return lax.dot_general(
            left_ref[...], right_ref[...], (dims, ((), ())), preferred_element_type=jnp.float32
        )

    d_first = product(d_joined_ref, qkv_ref, NT)
    d_second = product(d_hidden_ref, up_ref, NT)
    normed = normed_ref[...]
    width = normed.shape[1]
    sums_ref[0:1, :] = jnp.sum(d_first * normed, axis=0, keepdims=True)
    sums_ref[1:2, :] = jnp.sum(d_first, axis=0, keepdims=True)
    sums_ref[2:3, :] = jnp.sum(d_second * normed, axis=0, keepdims=True)
    sums_ref[3:4, :] = jnp.sum(d_second, axis=0, keepdims=True)
    mixed = d_first * affine_ref[0:1, :] + d_second * affine_ref[2:3, :]
    branch = product(flat_ref, out_ref, NN) + product(active_ref, down_ref, NN)
    half = keep_ref.shape[0]
    for start, part in ((0, mixed), (width, branch)):
        columns = slice(start, start + width)
        keep_ref[:, columns] = part[:half]
        send_ref[:, columns] = part[half:].astype(jnp.bfloat16)


def mix(d_joined, qkv_weight, d_hidden, up_weight, normed, affine, flat, out_weight, active, down):
    rows, width = normed.shape
    in_vmem = pl.BlockSpec(memory_space=pltpu.VMEM)
    return pl.pallas_call(
        mix_body,
        in_specs=[in_vmem] * 10,
        out_specs=[in_vmem] * 3,
        out_shape=[
            jax.ShapeDtypeStruct((rows // 2, 2 * width), jnp.float32),
            jax.ShapeDtypeStruct((rows // 2, 2 * width), jnp.bfloat16),
            jax.ShapeDtypeStruct((4, width), jnp.float32),
        ],
        compiler_params=pltpu.CompilerParams(vmem_limit_bytes=16 << 20),
        name="mix",
    )(d_joined, qkv_weight, d_hidden, up_weight, normed, affine, flat, out_weight, active, down)


def attention_body(
    first_ref,
    weight_ref,
    bias_ref,
    grad_ref,
    out_ref,
    ids_ref,
    lengths_ref,
    flat_ref,
    d_joined_ref,
    bias_sum_ref,
    turned_ref,
    d_turned_ref,
):
    heads = weight_ref.shape[1] // (3 * HD)
    half = ROT // 2
    scale = 1.0 / math.sqrt(HD)

    def columns(head, kind):
        start = (3 * head + kind) * HD
        return slice(start, start + HD)

    joined = (
        lax.dot_general(
            first_ref[...], weight_ref[...], (NN, ((), ())), preferred_element_type=jnp.float32
        )
        + bias_ref[...]
    )
    total = joined.shape[1]

    direct, later, earlier, mask = rotary_and_mask(ids_ref, lengths_ref, joined.shape[0])
    direct, later, earlier = (
        jnp.concatenate([part] * (heads // 2), axis=1) for part in (direct, later, earlier)
    )
    turned_ref[...] = (
        joined * direct
        + pltpu.roll(joined, total - half, 1) * later
        + pltpu.roll(joined, half, 1) * earlier
    ).astype(jnp.bfloat16)
    d_attended_all = lax.dot_general(
        grad_ref[...], out_ref[...], (NT, ((), ())), preferred_element_type=jnp.float32
    ).astype(jnp.bfloat16)

    def product(left, right, dims):
        return lax.dot_general(left, right, (dims, ((), ())), preferred_element_type=jnp.float32)

    for head in range(heads):
        query = turned_ref[:, columns(head, 0)]
        key = turned_ref[:, columns(head, 1)]
        value = turned_ref[:, columns(head, 2)]
        d_attended = d_attended_all[:, head * HD : (head + 1) * HD]
        scores = product(query, key, NT) * scale + mask
        peak = jnp.max(scores, axis=1, keepdims=True)
        expo = jnp.exp(scores - peak)
        probs = expo / jnp.sum(expo, axis=1, keepdims=True)
        probs_b = probs.astype(jnp.bfloat16)
        attended = product(probs_b, value, NN).astype(jnp.bfloat16)
        flat_ref[:, head * HD : (head + 1) * HD] = attended
        d_probs = product(d_attended, value, NT)
        delta = jnp.sum(
            d_attended.astype(jnp.float32) * attended.astype(jnp.float32), axis=1, keepdims=True
        )
        d_scores = (probs * (d_probs - delta) * scale).astype(jnp.bfloat16)
        d_turned_ref[:, columns(head, 0)] = product(d_scores, key, NN)
        d_turned_ref[:, columns(head, 1)] = product(d_scores, query, TN)
        d_turned_ref[:, columns(head, 2)] = product(probs_b, d_attended, TN)
    d_turned = d_turned_ref[...]
    d_joined = (
        d_turned * direct
        - pltpu.roll(d_turned, total - half, 1) * later
        - pltpu.roll(d_turned, half, 1) * earlier
    )
    bias_sum_ref[...] = jnp.sum(d_joined, axis=0, keepdims=True)
    d_joined_ref[...] = d_joined.astype(jnp.bfloat16)


def attention(first_in, weight, bias, grad_rows, out_weight, block_ids, lengths):
    rows = first_in.shape[0]
    columns = weight.shape[1]
    in_vmem = pl.BlockSpec(memory_space=pltpu.VMEM)
    return pl.pallas_call(
        attention_body,
        in_specs=[in_vmem] * 5 + [pl.BlockSpec(memory_space=pltpu.SMEM)] * 2,
        out_specs=[in_vmem] * 3,
        out_shape=[
            jax.ShapeDtypeStruct((rows, columns // 3), jnp.bfloat16),
            jax.ShapeDtypeStruct((rows, columns), jnp.bfloat16),
            jax.ShapeDtypeStruct((1, columns), jnp.float32),
        ],
        scratch_shapes=[
            pltpu.VMEM((rows, columns), jnp.bfloat16),
            pltpu.VMEM((rows, columns), jnp.float32),
        ],
        compiler_params=pltpu.CompilerParams(vmem_limit_bytes=16 << 20),
        name="attention",
    )(
        first_in,
        weight,
        bias[None, :],
        grad_rows,
        out_weight,
        block_ids,
        lengths,
    )


def normalize(inputs):
    centered = inputs - jnp.mean(inputs, axis=-1, keepdims=True)
    inv_std = lax.rsqrt(jnp.mean(centered * centered, axis=-1, keepdims=True) + epsilon)
    return (centered * inv_std, inv_std)


def swap(array, axis, bit):
    count = lax.axis_size(axis)
    return lax.ppermute(array, axis, [(i, i ^ (1 << bit)) for i in range(count)])


def axis_bits(axis):
    return lax.axis_size(axis).bit_length() - 1


def relatives(bits):
    found = [0]
    for bit in reversed(bits):
        found = found + [relative | (1 << bit) for relative in found]
    return found


def relative_blocks(array, axis, bits, dim):
    own = lax.axis_index(axis)
    size = array.shape[dim] // lax.axis_size(axis)
    pieces = [
        lax.dynamic_slice_in_dim(array, (own ^ relative) * size, size, dim)
        for relative in relatives(bits)
    ]
    return jnp.concatenate(pieces, axis=dim)


def fold(piece, axis, bits, dim):
    count = 1 << len(bits)
    send = piece(count // 2, count).astype(jnp.bfloat16)
    arrived = []
    for depth, bit in enumerate(bits):
        arrived.append((swap(send, axis, bit), count >> (depth + 1)))
        stop = count >> (depth + 1)
        last = depth + 1 == len(bits)
        total = piece(stop // 2, stop)
        for part, held in arrived[: -1 if last else None]:
            total = total + cut(part, dim, held, stop // 2, stop)
        send = total.astype(jnp.bfloat16)
    return lax.optimization_barrier(total) + arrived[-1][0]


def cut(array, dim, count, start, stop):
    size = array.shape[dim] // count
    return lax.slice_in_dim(array, start * size, stop * size, axis=dim)


def all_sum(array, axis, bits):
    for bit in bits:
        array = array + swap(array, axis, bit)
    return array


def dot(left, right, dims):
    return lax.dot_general(left, right, (dims, ((), ())), preferred_element_type=jnp.float32)


def shards(
    tokens,
    seq_lengths,
    ln1_gain,
    ln1_bias,
    ln2_gain,
    ln2_bias,
    qkv_weight,
    qkv_bias,
    out_weight,
    out_bias,
    up_weight,
    up_bias,
    down_weight,
    down_bias,
    cotangent,
):
    row_count = tokens.shape[0]
    width = tokens.shape[1]
    tensor_bits = list(range(axis_bits("tensor")))
    dp_bits = list(range(axis_bits("dp")))
    y_first = dp_bits
    z_first = dp_bits[1:2] + dp_bits[0:1] + dp_bits[2:]
    own_rank = lax.axis_index("tensor")
    block_ids = (own_rank ^ jnp.array(relatives(tensor_bits), jnp.int32)) * row_count

    def gather(rows):
        pieces = [rows]
        for bit in reversed(tensor_bits):
            arrived = []
            for piece in pieces:
                arrived.append(swap(piece, "tensor", bit))
            pieces = pieces + arrived
        return pieces

    token_pieces = gather(tokens)
    grad_pieces = gather(cotangent)
    own_group = lax.axis_index("dp")
    places = own_group ^ jnp.array(relatives(y_first) + relatives(z_first), jnp.int32)
    affine = jnp.stack(
        [ln1_gain, ln1_bias, ln2_gain, ln2_bias, *up_bias.reshape(-1, width)]
    )
    affine = pack(affine, up_weight)
    groups = lax.axis_size("dp")
    relative = width // groups == 128
    second_in, active, slope, *second_rel = front(places, token_pieces, affine, up_weight, relative)
    grad_rows_all, *grad_y = join(places, grad_pieces, relative)
    first_in, whole_normed, inv_std, bias_total, *rest = norm(
        places, token_pieces, affine, grad_rows_all, relative
    )
    bias_total = bias_total[0]
    normed = whole_normed[:row_count]
    if relative:
        (grad_y,) = grad_y
        (second_rel,) = second_rel
        first_rel, grad_z = rest
    else:
        grad_y = relative_blocks(grad_rows_all, "dp", y_first, 1)
        first_rel = relative_blocks(first_in, "dp", y_first, 1)
        second_rel = relative_blocks(second_in, "dp", z_first, 1)
        grad_z = relative_blocks(grad_rows_all, "dp", z_first, 1)

    def by_columns(left, right):
        return lambda start, stop: dot(left, cut(right, 1, groups, start, stop), TN)

    def by_rows(left, right):
        return lambda start, stop: dot(cut(left, 1, groups, start, stop), right, TN)

    grad_down_weight = fold(by_columns(active, grad_y), "dp", y_first, 1)
    d_hidden = dot(grad_rows_all, down_weight, NT) * slope
    d_hidden_b = d_hidden.astype(jnp.bfloat16)
    g_up_bias = jnp.sum(d_hidden, axis=0)
    grad_up_weight = fold(by_rows(second_rel, d_hidden_b), "dp", z_first, 0)

    flat, d_joined_b, g_qkv_bias = attention(
        first_in,
        qkv_weight,
        qkv_bias,
        grad_rows_all,
        out_weight,
        block_ids,
        seq_lengths,
    )
    g_qkv_bias = g_qkv_bias[0]
    grad_qkv_weight = fold(by_rows(first_rel, d_joined_b), "dp", y_first, 0)
    grad_out_weight = fold(by_columns(flat, grad_z), "dp", z_first, 1)

    members = lax.axis_size("tensor")
    keep, send, norm_sums = mix(
        d_joined_b,
        qkv_weight,
        d_hidden_b,
        up_weight,
        whole_normed,
        affine,
        flat,
        out_weight,
        active,
        down_weight,
    )

    def token_piece(start, stop):
        if stop == members:
            return send
        return cut(keep, 0, members // 2, start, stop)

    both = fold(token_piece, "tensor", tensor_bits, 0)
    mixed = both[:, :width]
    branch = both[:, width:]
    norm_sums = all_sum(norm_sums.reshape(-1), "tensor", tensor_bits)
    sums = all_sum(
        jnp.concatenate([norm_sums, bias_total, g_up_bias, g_qkv_bias]),
        "dp",
        dp_bits[:1] + dp_bits[:0:-1],
    )
    gain_one, shift_one, gain_two, shift_two, bias_total = (
        sums[i * width : (i + 1) * width] for i in range(5)
    )
    rest = sums[5 * width :]
    grad_up_bias = rest[: g_up_bias.shape[0]]
    grad_qkv_bias = rest[g_up_bias.shape[0] :]

    rows_float = tokens.astype(jnp.float32)
    output = (rows_float + branch + out_bias + down_bias).astype(jnp.bfloat16)
    grad_float = cotangent.astype(jnp.float32)
    grad_input = (
        inv_std
        * (
            mixed
            - jnp.mean(mixed, axis=-1, keepdims=True)
            - normed * jnp.mean(mixed * normed, axis=-1, keepdims=True)
        )
        + grad_float
    )
    grad_input = grad_input.astype(jnp.bfloat16)
    return (
        output,
        grad_input,
        gain_one,
        shift_one,
        gain_two,
        shift_two,
        grad_qkv_weight,
        grad_qkv_bias,
        grad_out_weight,
        bias_total,
        grad_up_weight,
        grad_up_bias,
        grad_down_weight,
        bias_total,
    )


def solution(mesh):
    placed = (
        P(("dp", "tensor"), None),
        P("dp", None),
        P(),
        P(),
        P(),
        P(),
        P(None, "tensor"),
        P("tensor"),
        P("tensor", None),
        P(),
        P(None, "tensor"),
        P("tensor"),
        P("tensor", None),
        P(),
        P(("dp", "tensor"), None),
    )
    return jax.shard_map(
        shards,
        mesh=mesh,
        in_specs=placed,
        out_specs=(
            P(("dp", "tensor"), None),
            P(("dp", "tensor"), None),
            P(),
            P(),
            P(),
            P(),
            P("dp", "tensor"),
            P("tensor"),
            P("tensor", "dp"),
            P(),
            P("dp", "tensor"),
            P("tensor"),
            P("tensor", "dp"),
            P(),
        ),
        check_vma=False,
    )
```

time: 156 us -> 156 us (level)
  other arithmetic: 15.6 us -> 4.6 us
  Pallas kernels: 10.6 us -> 19.5 us
  local copies, waits for them, and re-layouts: 14.7 us -> 8.82 us
  waiting for transfers between devices: 62.9 us -> 67.8 us
  matrix products: 19.6 us -> 24.1 us
  starting transfers between devices: 31.3 us -> 29.1 us
    pallas_call x1 -> x6, Pallas kernels: 10.6 us -> 19.5 us  [the longest x1 7.49 us: attention(): pl.pallas_call(attention_body, in_specs=[in_vmem] * 5 + [pl.BlockSpec(mem...]
    concatenate x4 -> x0, local copies, waits for them, and re-layouts: 5.34 us -> none  [the longest x3 5.31 us: rotary_tables(): jnp.concatenate(part + part + [last], axis=1)]
    ppermute x25, waiting for transfers between devices: 62.9 us -> 67.8 us  [swap(): return lax.ppermute(array, axis, [(i, i ^ 1 << bit) for i in range(count)])]
    dot_general x14 -> x17, matrix products: 19.6 us -> 24.1 us  [dot(): lax.dot_general(left, right, (dims, ((), ())), preferred_element_type=jnp...]
    unnamed x109 -> x58, local copies, waits for them, and re-layouts: 1.79 us -> 6.14 us
    reduce_sum x7 -> x0, other arithmetic: 3.05 us -> none  [the longest x2 1.49 us: normalize(): jnp.mean(centered * centered, axis=-1, keepdims=True) + epsilon]
    concatenate x4 -> x0, other arithmetic: 2.89 us -> none  [the longest x2 2.81 us: gather(): rows = jnp.concatenate([rows, swap(rows, 'tensor', bit)], axis=0)]
    dynamic_slice x2 -> x0, local copies, waits for them, and re-layouts: 2.27 us -> none  [relative_blocks(): lax.dynamic_slice_in_dim(array, (own ^ relative) * size, size, dim)]
  transfers between devices with their start and end apart: 25 -> 25, of which waited for: 13 -> 12; matrix products, arithmetic and copies ran while one was open for 24% -> 19% of each run, Pallas kernels for 0% -> 1%
where the time goes in v1:
time: 156 us; the launch traced here: 155 us
  waiting for transfers between devices  67.8 us (43%)
  starting transfers between devices  29.1 us (19%)
  matrix products  24.1 us (15%)
  Pallas kernels  19.5 us (12%)
  local copies, waits for them, and re-layouts  8.82 us (6%)
  other arithmetic  4.6 us (3%)
    ppermute x25, waiting for transfers between devices, swap(): return lax.ppermute(array, axis, [(i, i ^ 1 << bit) for i in range(count)])  67.8 us
    ppermute x25, starting transfers between devices, swap(): return lax.ppermute(array, axis, [(i, i ^ 1 << bit) for i in range(count)])  29.1 us
    dot_general x17, matrix products, dot(): lax.dot_general(left, right, (dims, ((), ())), preferred_element_type=jnp...  24.1 us
    pallas_call x1, Pallas kernels, attention(): pl.pallas_call(attention_body, in_specs=[in_vmem] * 5 + [pl.BlockSpec(mem...  7.49 us
    unnamed x58, local copies, waits for them, and re-layouts  6.14 us
    pallas_call x1, Pallas kernels, front(): pl.pallas_call(lambda *refs: front_body(*refs, blocks=len(pieces), relati...  4.16 us
    add x5, other arithmetic, fold(): return lax.optimization_barrier(total) + arrived[-1][0]  3.23 us
    pallas_call x1, Pallas kernels, norm(): pl.pallas_call(lambda *refs: norm_body(*refs, blocks=len(pieces), relativ...  3.19 us
  transfers between devices with their start and end apart: 25, of which 12 were waited for; matrix products, arithmetic and copies ran while one was open for 19% of the time, Pallas kernels for 1%

profile of v1, /device:TPU:0, one launch (start us, length us, event | category | flops | bytes accessed | tf_op | source)
XLA Modules:
  0.0 155.2 jit_solution(4076369697373412300)
XLA Ops:
  0.7 3.0 %collective-permute-start = (bf16[96,1024]{1,0:T(8,128)(2,1)}, bf16[96,1024]{1,0:T(8,128)(2,1)S(1)}, u32[]{:S(2)}, u32[]{:S(2)}) collective-permute-start(bf16[96,1024]{1,0:T(8,128)(2,1)} %refs_1_.5), channel_id=1, source_target_pairs={{0,2},{1,3},{2,0},{3,1},{4,6},{5,7},{6,4},{7,5},{8,10},{9,11},{10,... | collective-permute-start | bytes 589832 | tf_op jit(solution)/shard_map/ppermute | solution.py:414
  7.3 2.3 %collective-permute-done.refs_2_ = bf16[96,1024]{1,0:T(8,128)(2,1)S(1)} collective-permute-done((bf16[96,1024]{1,0:T(8,128)(2,1)}, bf16[96,1024]{1,0:T(8,128)(2,1)S(1)}, u32[]{:S(2)}, u32[]{:S(2)}) %collective-permute-start) | collective-permute-done | bytes 196640 | tf_op jit(solution)/shard_map/ppermute | solution.py:414
  9.7 3.4 %collective-permute-done.3.refs_2_ = bf16[96,1024]{1,0:T(8,128)(2,1)S(1)} collective-permute-done((bf16[96,1024]{1,0:T(8,128)(2,1)}, bf16[96,1024]{1,0:T(8,128)(2,1)S(1)}, u32[]{:S(2)}, u32[]{:S(2)}) %collective-permute-start.3) | collective-permute-done | bytes 196640 | tf_op jit(solution)/shard_map/ppermute | solution.py:414
  15.4 1.8 %join.1 = (bf16[384,1024]{1,0:T(8,128)(2,1)S(1)}, bf16[384,1024]{1,0:T(8,128)(2,1)S(1)}) custom-call(s32[16]{0:T(128)S(1)} %broadcast_xor_fusion.refs_0_, bf16[96,1024]{1,0:T(8,128)(2,1)S(1)} %copy-done.10, bf16[96,1024]{1,0:T(8,128)(2,1)S(1)} %collective-permute-done.3.refs_2_, bf16[96,1024]{1,0:T(8,128)(2,1)S(1)} %collective-permute-done.4.refs_3_, ...), custom_call_target="tpu_custom_call" | custom-call | tf_op jit(solution)/shard_map/join/pallas_call | solution.py:185
  17.3 4.2 %front.1 = (bf16[384,1024]{1,0:T(8,128)(2,1)}, bf16[384,1024]{1,0:T(8,128)(2,1)S(1)}, f32[384,1024]{1,0:T(8,128)S(1)}, bf16[384,1024]{1,0:T(8,128)(2,1)S(1)}) custom-call(s32[16]{0:T(128)S(1)} %broadcast_xor_fusion.refs_0_, bf16[96,1024]{1,0:T(8,128)(2,1)S(1)} %copy-done.7, bf16[96,1024]{1,0:T(8,128)(2,1)S(1)} %collective-permute-done.refs_2_, ...), custom_call_target="tpu_custom_call" | custom-call | tf_op jit(solution)/shard_map/front/pallas_call | solution.py:153
  23.4 3.2 %norm.1 = (bf16[384,1024]{1,0:T(8,128)(2,1)S(1)}, f32[384,1024]{1,0:T(8,128)S(1)}, f32[96,1]{1,0:T(8,128)S(1)}, f32[1,1024]{1,0:T(1,128)S(1)}, bf16[384,1024]{1,...) custom-call(s32[16]{0:T(128)S(1)} %broadcast_xor_fusion.refs_0_, bf16[96,1024]{1,0:T(8,128)(2,1)S(1)} %copy-done.7, ...), custom_call_target="tpu_custom_call" | custom-call | tf_op jit(solution)/shard_map/norm/pallas_call | solution.py:232
  27.6 7.5 %attention.1 = (bf16[384,256]{1,0:T(8,128)(2,1)S(1)}, bf16[384,768]{1,0:T(8,128)(2,1)S(1)}, f32[1,768]{1,0:T(1,128)S(1)}) custom-call(bf16[384,1024]{1,0:T(8,128)(2,1)S(1)} %get-tuple-element.32.first_ref, bf16[1024,768]{1,0:T(8,128)(2,1)S(1)} %copy-done.3, f32[1,768]{1,0:T(1,128)S(1)} %broadcast_in_dim.2.bias_ref, ...), custom_call_target="tpu_custom_call" | custom-call | tf_op jit(solution)/shard_map/attention/pallas_call | solution.py:380
  35.1 2.9 %mix.1 = (f32[192,2048]{1,0:T(8,128)S(1)}, bf16[192,2048]{1,0:T(8,128)(2,1)S(1)}, f32[4,1024]{1,0:T(4,128)S(1)}) custom-call(bf16[384,768]{1,0:T(8,128)(2,1)S(1)} %get-tuple-element.33.d_joined_ref, bf16[1024,768]{1,0:T(8,128)(2,1)S(1)} %copy-done.3, bf16[384,1024]{1,0:T(8,128)(2,1)S(1)} %get-tuple-element.53.d_hidden_ref, bf16[1024,1024]{1,0:T(8,128)(2,1)S(1)} %copy-done.1, ...), custom_call_target="tpu_custom_call" | custom-call | tf_op jit(solution)/shard_map/mix/pallas_call | solution.py:286
  39.2 1.7 %collective-permute-start.9 = (f32[4096]{0:T(1024)S(1)}, f32[4096]{0:T(1024)S(1)}, u32[]{:S(2)}, u32[]{:S(2)}) collective-permute-start(f32[4096]{0:T(1024)S(1)} %fusion.35), channel_id=1, source_target_pairs={{0,2},{1,3},{2,0},{3,1},{4,6},{5,7},{6,4},{7,5},{8,10},{9,11},{10,... | collective-permute-start | bytes 49160 | tf_op jit(solution)/shard_map/ppermute | solution.py:414
  41.0 1.8 %convolution_convert_fusion = bf16[1024,512]{1,0:T(8,128)(2,1)} fusion(bf16[384,1024]{1,0:T(8,128)(2,1)S(1)} %get-tuple-element.37.active_ref, bf16[384,1024]{1,0:T(8,128)(2,1)S(1)} %get-tuple-element.47), kind=kOutput, calls=%fused_computation | convolution fusion | flops 403177472 | bytes 2228224 | tf_op jit(solution)/shard_map/dot_general | solution.py:465
  44.9 2.8 %convolution_convert_fusion.1 = bf16[512,1024]{1,0:T(8,128)(2,1)} fusion(bf16[384,1024]{1,0:T(8,128)(2,1)S(1)} %get-tuple-element.53.d_hidden_ref, bf16[384,1024]{1,0:T(8,128)(2,1)} %copy-done.15), kind=kOutput, calls=%fused_computation.1 | convolution fusion | flops 403177472 | bytes 2228224 | tf_op jit(solution)/shard_map/dot_general | solution.py:465
  49.3 19.3 %collective-permute-done.10 = f32[6912]{0:T(1024)S(1)} collective-permute-done((f32[6912]{0:T(1024)S(1)}, f32[6912]{0:T(1024)S(1)}, u32[]{:S(2)}, u32[]{:S(2)}) %collective-permute-start.10) | collective-permute-done | bytes 27680 | tf_op jit(solution)/shard_map/ppermute | solution.py:414
  68.5 2.6 %collective-permute-start.11 = (f32[6912]{0:T(1024)S(1)}, f32[6912]{0:T(1024)S(1)}, u32[]{:S(2)}, u32[]{:S(2)}) collective-permute-start(f32[6912]{0:T(1024)S(1)} %fusion.36), channel_id=1, source_target_pairs={{0,16},{4,20},{8,24},{12,28},{16,0},{20,4},{24,8},{28,12},{1,17},{... | collective-permute-start | bytes 82952 | tf_op jit(solution)/shard_map/ppermute | solution.py:414
  73.7 3.1 %collective-permute-start.12 = (f32[6912]{0:T(1024)S(1)}, f32[6912]{0:T(1024)S(1)}, u32[]{:S(2)}, u32[]{:S(2)}) collective-permute-start(f32[6912]{0:T(1024)S(1)} %add.130), channel_id=1, source_target_pairs={{0,8},{4,12},{8,0},{12,4},{16,24},{20,28},{24,16},{28,20},{1,9},{5... | collective-permute-start | bytes 82952 | tf_op jit(solution)/shard_map/ppermute | solution.py:414
  84.3 13.0 %collective-permute-done.17 = bf16[256,256]{1,0:T(8,128)(2,1)S(1)} collective-permute-done((bf16[256,256]{1,0:T(8,128)(2,1)S(1)}, bf16[256,256]{1,0:T(8,128)(2,1)S(1)}, u32[]{:S(2)}, u32[]{:S(2)}) %collective-permute-start.17) | collective-permute-done | bytes 131104 | tf_op jit(solution)/shard_map/ppermute | solution.py:414
  98.5 2.2 %collective-permute-start.18 = (bf16[256,128]{1,0:T(8,128)(2,1)S(1)}, bf16[256,128]{1,0:T(8,128)(2,1)S(1)}, u32[]{:S(2)}, u32[]{:S(2)}) collective-permute-start(bf16[256,128]{1,0:T(8,128)(2,1)S(1)} %fusion.15), channel_id=1, source_target_pairs={{0,16},{4,20},{8,24},{12,28},{16,0},{20,4},{24,8},{28,12},{1,17},{... | collective-permute-start | bytes 196616 | tf_op jit(solution)/shard_map/ppermute | solution.py:414
  101.9 2.6 %collective-permute-done.18 = bf16[256,128]{1,0:T(8,128)(2,1)S(1)} collective-permute-done((bf16[256,128]{1,0:T(8,128)(2,1)S(1)}, bf16[256,128]{1,0:T(8,128)(2,1)S(1)}, u32[]{:S(2)}, u32[]{:S(2)}) %collective-permute-start.18) | collective-permute-done | bytes 65568 | tf_op jit(solution)/shard_map/ppermute | solution.py:414
  109.6 2.0 %collective-permute-start.23 = (bf16[1024,256]{1,0:T(8,128)(2,1)S(1)}, bf16[1024,256]{1,0:T(8,128)(2,1)S(1)}, u32[]{:S(2)}, u32[]{:S(2)}) collective-permute-start(bf16[1024,256]{1,0:T(8,128)(2,1)S(1)} %fusion.1), channel_id=1, source_target_pairs={{0,8},{4,12},{8,0},{12,4},{16,24},{20,28},{24,16},{28,20},{1,9},{5... | collective-permute-start | bytes 1572872 | tf_op jit(solution)/shard_map/ppermute | solution.py:414
  113.1 1.6 %collective-permute-start.20 = (bf16[256,1024]{1,0:T(8,128)(2,1)S(1)}, bf16[256,1024]{1,0:T(8,128)(2,1)S(1)}, u32[]{:S(2)}, u32[]{:S(2)}) collective-permute-start(bf16[256,1024]{1,0:T(8,128)(2,1)S(1)} %fusion), channel_id=1, source_target_pairs={{0,4},{4,0},{8,12},{12,8},{16,20},{20,16},{24,28},{28,24},{1,5},{5... | collective-permute-start | bytes 1572872 | tf_op jit(solution)/shard_map/ppermute | solution.py:414
  114.7 6.0 %collective-permute-done.14 = bf16[256,768]{1,0:T(8,128)(2,1)S(1)} collective-permute-done((bf16[256,768]{1,0:T(8,128)(2,1)S(1)}, bf16[256,768]{1,0:T(8,128)(2,1)S(1)}, u32[]{:S(2)}, u32[]{:S(2)}) %collective-permute-start.14) | collective-permute-done | bytes 393248 | tf_op jit(solution)/shard_map/ppermute | solution.py:414
  125.0 12.5 %collective-permute-done.15 = bf16[128,768]{1,0:T(8,128)(2,1)S(1)} collective-permute-done((bf16[128,768]{1,0:T(8,128)(2,1)S(1)}, bf16[128,768]{1,0:T(8,128)(2,1)S(1)}, u32[]{:S(2)}, u32[]{:S(2)}) %collective-permute-start.15) | collective-permute-done | bytes 196640 | tf_op jit(solution)/shard_map/ppermute | solution.py:414
  141.0 3.0 %collective-permute-start.21 = (bf16[128,1024]{1,0:T(8,128)(2,1)S(1)}, bf16[128,1024]{1,0:T(8,128)(2,1)S(1)}, u32[]{:S(2)}, u32[]{:S(2)}) collective-permute-start(bf16[128,1024]{1,0:T(8,128)(2,1)S(1)} %fusion.7), channel_id=1, source_target_pairs={{0,16},{4,20},{8,24},{12,28},{16,0},{20,4},{24,8},{28,12},{1,17},{... | collective-permute-start | bytes 786440 | tf_op jit(solution)/shard_map/ppermute | solution.py:414
  146.6 4.3 %collective-permute-done.24 = bf16[1024,128]{1,0:T(8,128)(2,1)S(1)} collective-permute-done((bf16[1024,128]{1,0:T(8,128)(2,1)S(1)}, bf16[1024,128]{1,0:T(8,128)(2,1)S(1)}, u32[]{:S(2)}, u32[]{:S(2)}) %collective-permute-start.24) | collective-permute-done | bytes 262176 | tf_op jit(solution)/shard_map/ppermute | solution.py:414
  151.8 2.0 %collective-permute-done.21 = bf16[128,1024]{1,0:T(8,128)(2,1)S(1)} collective-permute-done((bf16[128,1024]{1,0:T(8,128)(2,1)S(1)}, bf16[128,1024]{1,0:T(8,128)(2,1)S(1)}, u32[]{:S(2)}, u32[]{:S(2)}) %collective-permute-start.21) | collective-permute-done | bytes 262176 | tf_op jit(solution)/shard_map/ppermute | solution.py:414
  (130 shorter events, 45.5 us)
Async XLA Ops:
  0.7 9.0 %collective-permute-start = (bf16[96,1024]{1,0:T(8,128)(2,1)}, bf16[96,1024]{1,0:T(8,128)(2,1)S(1)}, u32[]{:S(2)}, u32[]{:S(2)}) collective-permute-start(bf16[96,1024]{1,0:T(8,128)(2,1)} %refs_1_.5), channel_id=1, source_target_pairs={{0,2},{1,3},{2,0},{3,1},{4,6},{5,7},{6,4},{7,5},{8,10},{9,11},{10,... | collective-permute-start | bytes 589832 | tf_op jit(solution)/shard_map/ppermute | solution.py:414
  3.7 13.5 %collective-permute-start.1 = (bf16[96,1024]{1,0:T(8,128)(2,1)}, bf16[96,1024]{1,0:T(8,128)(2,1)S(1)}, u32[]{:S(2)}, u32[]{:S(2)}) collective-permute-start(bf16[96,1024]{1,0:T(8,128)(2,1)} %refs_1_.5), channel_id=1, source_target_pairs={{0,1},{1,0},{2,3},{3,2},{4,5},{5,4},{6,7},{7,6},{8,9},{9,8},{10,11... | collective-permute-start | bytes 589832 | tf_op jit(solution)/shard_map/ppermute | solution.py:414
  3.7 9.3 %collective-permute-start.3 = (bf16[96,1024]{1,0:T(8,128)(2,1)}, bf16[96,1024]{1,0:T(8,128)(2,1)S(1)}, u32[]{:S(2)}, u32[]{:S(2)}) collective-permute-start(bf16[96,1024]{1,0:T(8,128)(2,1)} %refs_1_.3), channel_id=1, source_target_pairs={{0,2},{1,3},{2,0},{3,1},{4,6},{5,7},{6,4},{7,5},{8,10},{9,11},{10,... | collective-permute-start | bytes 589832 | tf_op jit(solution)/shard_map/ppermute | solution.py:414
  3.9 9.2 %collective-permute-start.4 = (bf16[96,1024]{1,0:T(8,128)(2,1)}, bf16[96,1024]{1,0:T(8,128)(2,1)S(1)}, u32[]{:S(2)}, u32[]{:S(2)}) collective-permute-start(bf16[96,1024]{1,0:T(8,128)(2,1)} %refs_1_.3), channel_id=1, source_target_pairs={{0,1},{1,0},{2,3},{3,2},{4,5},{5,4},{6,7},{7,6},{8,9},{9,8},{10,11... | collective-permute-start | bytes 589832 | tf_op jit(solution)/shard_map/ppermute | solution.py:414
  9.7 7.6 %collective-permute-start.2 = (bf16[96,1024]{1,0:T(8,128)(2,1)S(1)}, bf16[96,1024]{1,0:T(8,128)(2,1)S(1)}, u32[]{:S(2)}, u32[]{:S(2)}) collective-permute-start(bf16[96,1024]{1,0:T(8,128)(2,1)S(1)} %collective-permute-done.refs_2_), channel_id=1, source_target_pairs={{0,1},{1,0},{2,3},{3,2},{4,5},{5,4},{6,7},{7,6},{8,9},{9,8},{10,11... | collective-permute-start | bytes 589832 | tf_op jit(solution)/shard_map/ppermute | solution.py:414
  13.0 1.4 collective-permute-start.5
  39.2 5.1 %collective-permute-start.9 = (f32[4096]{0:T(1024)S(1)}, f32[4096]{0:T(1024)S(1)}, u32[]{:S(2)}, u32[]{:S(2)}) collective-permute-start(f32[4096]{0:T(1024)S(1)} %fusion.35), channel_id=1, source_target_pairs={{0,2},{1,3},{2,0},{3,1},{4,6},{5,7},{6,4},{7,5},{8,10},{9,11},{10,... | collective-permute-start | bytes 49160 | tf_op jit(solution)/shard_map/ppermute | solution.py:414
  42.8 64.8 %collective-permute-start.22 = (bf16[1024,512]{1,0:T(8,128)(2,1)}, bf16[1024,512]{1,0:T(8,128)(2,1)}, u32[]{:S(2)}, u32[]{:S(2)}) collective-permute-start(bf16[1024,512]{1,0:T(8,128)(2,1)} %convolution_convert_fusion), channel_id=1, source_target_pairs={{0,4},{4,0},{8,12},{12,8},{16,20},{20,16},{24,28},{28,24},{1,5},{5... | collective-permute-start | bytes 3145736 | tf_op jit(solution)/shard_map/ppermute | solution.py:414
  44.3 24.2 %collective-permute-start.10 = (f32[6912]{0:T(1024)S(1)}, f32[6912]{0:T(1024)S(1)}, u32[]{:S(2)}, u32[]{:S(2)}) collective-permute-start(f32[6912]{0:T(1024)S(1)} %pad_maximum_fusion), channel_id=1, source_target_pairs={{0,4},{4,0},{8,12},{12,8},{16,20},{20,16},{24,28},{28,24},{1,5},{5... | collective-permute-start | bytes 82952 | tf_op jit(solution)/shard_map/ppermute | solution.py:414
  47.7 63.9 %collective-permute-start.19 = (bf16[512,1024]{1,0:T(8,128)(2,1)}, bf16[512,1024]{1,0:T(8,128)(2,1)}, u32[]{:S(2)}, u32[]{:S(2)}) collective-permute-start(bf16[512,1024]{1,0:T(8,128)(2,1)} %convolution_convert_fusion.1), channel_id=1, source_target_pairs={{0,8},{4,12},{8,0},{12,4},{16,24},{20,28},{24,16},{28,20},{1,9},{5... | collective-permute-start | bytes 3145736 | tf_op jit(solution)/shard_map/ppermute | solution.py:414
  68.5 5.2 %collective-permute-start.11 = (f32[6912]{0:T(1024)S(1)}, f32[6912]{0:T(1024)S(1)}, u32[]{:S(2)}, u32[]{:S(2)}) collective-permute-start(f32[6912]{0:T(1024)S(1)} %fusion.36), channel_id=1, source_target_pairs={{0,16},{4,20},{8,24},{12,28},{16,0},{20,4},{24,8},{28,12},{1,17},{... | collective-permute-start | bytes 82952 | tf_op jit(solution)/shard_map/ppermute | solution.py:414
  72.1 7.9 %collective-permute-start.16 = (bf16[256,512]{1,0:T(8,128)(2,1)}, bf16[256,512]{1,0:T(8,128)(2,1)}, u32[]{:S(2)}, u32[]{:S(2)}) collective-permute-start(bf16[256,512]{1,0:T(8,128)(2,1)} %convolution_convert_fusion.3), channel_id=1, source_target_pairs={{0,8},{4,12},{8,0},{12,4},{16,24},{20,28},{24,16},{28,20},{1,9},{5... | collective-permute-start | bytes 786440 | tf_op jit(solution)/shard_map/ppermute | solution.py:414
  73.7 6.3 %collective-permute-start.12 = (f32[6912]{0:T(1024)S(1)}, f32[6912]{0:T(1024)S(1)}, u32[]{:S(2)}, u32[]{:S(2)}) collective-permute-start(f32[6912]{0:T(1024)S(1)} %add.130), channel_id=1, source_target_pairs={{0,8},{4,12},{8,0},{12,4},{16,24},{20,28},{24,16},{28,20},{1,9},{5... | collective-permute-start | bytes 82952 | tf_op jit(solution)/shard_map/ppermute | solution.py:414
  78.3 26.8 %collective-permute-start.13 = (bf16[512,768]{1,0:T(8,128)(2,1)}, bf16[512,768]{1,0:T(8,128)(2,1)}, u32[]{:S(2)}, u32[]{:S(2)}) collective-permute-start(bf16[512,768]{1,0:T(8,128)(2,1)} %convolution_convert_fusion.2), channel_id=1, source_target_pairs={{0,4},{4,0},{8,12},{12,8},{16,20},{20,16},{24,28},{28,24},{1,5},{5... | collective-permute-start | bytes 2359304 | tf_op jit(solution)/shard_map/ppermute | solution.py:414
  80.0 26.7 %collective-permute-start.6 = (bf16[192,2048]{1,0:T(8,128)(2,1)}, bf16[192,2048]{1,0:T(8,128)(2,1)S(1)}, u32[]{:S(2)}, u32[]{:S(2)}) collective-permute-start(bf16[192,2048]{1,0:T(8,128)(2,1)} %copy-done.22), channel_id=1, source_target_pairs={{0,1},{1,0},{2,3},{3,2},{4,5},{5,4},{6,7},{7,6},{8,9},{9,8},{10,11... | collective-permute-start | bytes 2359304 | tf_op jit(solution)/shard_map/ppermute | solution.py:414
  81.6 15.7 %collective-permute-start.17 = (bf16[256,256]{1,0:T(8,128)(2,1)S(1)}, bf16[256,256]{1,0:T(8,128)(2,1)S(1)}, u32[]{:S(2)}, u32[]{:S(2)}) collective-permute-start(bf16[256,256]{1,0:T(8,128)(2,1)S(1)} %fusion.12), channel_id=1, source_target_pairs={{0,4},{4,0},{8,12},{12,8},{16,20},{20,16},{24,28},{28,24},{1,5},{5... | collective-permute-start | bytes 393224 | tf_op jit(solution)/shard_map/ppermute | solution.py:414
  98.5 5.9 %collective-permute-start.18 = (bf16[256,128]{1,0:T(8,128)(2,1)S(1)}, bf16[256,128]{1,0:T(8,128)(2,1)S(1)}, u32[]{:S(2)}, u32[]{:S(2)}) collective-permute-start(bf16[256,128]{1,0:T(8,128)(2,1)S(1)} %fusion.15), channel_id=1, source_target_pairs={{0,16},{4,20},{8,24},{12,28},{16,0},{20,4},{24,8},{28,12},{1,17},{... | collective-permute-start | bytes 196616 | tf_op jit(solution)/shard_map/ppermute | solution.py:414
  106.5 14.2 %collective-permute-start.14 = (bf16[256,768]{1,0:T(8,128)(2,1)S(1)}, bf16[256,768]{1,0:T(8,128)(2,1)S(1)}, u32[]{:S(2)}, u32[]{:S(2)}) collective-permute-start(bf16[256,768]{1,0:T(8,128)(2,1)S(1)} %fusion.2), channel_id=1, source_target_pairs={{0,8},{4,12},{8,0},{12,4},{16,24},{20,28},{24,16},{28,20},{1,9},{5... | collective-permute-start | bytes 1179656 | tf_op jit(solution)/shard_map/ppermute | solution.py:414
  106.9 15.1 %collective-permute-start.7 = (bf16[96,2048]{1,0:T(8,128)(2,1)S(1)}, bf16[96,2048]{1,0:T(8,128)(2,1)S(1)}, u32[]{:S(2)}, u32[]{:S(2)}) collective-permute-start(bf16[96,2048]{1,0:T(8,128)(2,1)S(1)} %get-tuple-element.50), channel_id=1, source_target_pairs={{0,2},{1,3},{2,0},{3,1},{4,6},{5,7},{6,4},{7,5},{8,10},{9,11},{10,... | collective-permute-start | bytes 1179656 | tf_op jit(solution)/shard_map/ppermute | solution.py:414
  109.6 28.6 %collective-permute-start.23 = (bf16[1024,256]{1,0:T(8,128)(2,1)S(1)}, bf16[1024,256]{1,0:T(8,128)(2,1)S(1)}, u32[]{:S(2)}, u32[]{:S(2)}) collective-permute-start(bf16[1024,256]{1,0:T(8,128)(2,1)S(1)} %fusion.1), channel_id=1, source_target_pairs={{0,8},{4,12},{8,0},{12,4},{16,24},{20,28},{24,16},{28,20},{1,9},{5... | collective-permute-start | bytes 1572872 | tf_op jit(solution)/shard_map/ppermute | solution.py:414
  113.1 26.6 %collective-permute-start.20 = (bf16[256,1024]{1,0:T(8,128)(2,1)S(1)}, bf16[256,1024]{1,0:T(8,128)(2,1)S(1)}, u32[]{:S(2)}, u32[]{:S(2)}) collective-permute-start(bf16[256,1024]{1,0:T(8,128)(2,1)S(1)} %fusion), channel_id=1, source_target_pairs={{0,4},{4,0},{8,12},{12,8},{16,20},{20,16},{24,28},{28,24},{1,5},{5... | collective-permute-start | bytes 1572872 | tf_op jit(solution)/shard_map/ppermute | solution.py:414
  121.9 15.5 %collective-permute-start.15 = (bf16[128,768]{1,0:T(8,128)(2,1)S(1)}, bf16[128,768]{1,0:T(8,128)(2,1)S(1)}, u32[]{:S(2)}, u32[]{:S(2)}) collective-permute-start(bf16[128,768]{1,0:T(8,128)(2,1)S(1)} %fusion.11), channel_id=1, source_target_pairs={{0,16},{4,20},{8,24},{12,28},{16,0},{20,4},{24,8},{28,12},{1,17},{... | collective-permute-start | bytes 589832 | tf_op jit(solution)/shard_map/ppermute | solution.py:414
  139.6 11.3 %collective-permute-start.24 = (bf16[1024,128]{1,0:T(8,128)(2,1)S(1)}, bf16[1024,128]{1,0:T(8,128)(2,1)S(1)}, u32[]{:S(2)}, u32[]{:S(2)}) collective-permute-start(bf16[1024,128]{1,0:T(8,128)(2,1)S(1)} %fusion.8), channel_id=1, source_target_pairs={{0,16},{4,20},{8,24},{12,28},{16,0},{20,4},{24,8},{28,12},{1,17},{... | collective-permute-start | bytes 786440 | tf_op jit(solution)/shard_map/ppermute | solution.py:414
  141.0 12.8 %collective-permute-start.21 = (bf16[128,1024]{1,0:T(8,128)(2,1)S(1)}, bf16[128,1024]{1,0:T(8,128)(2,1)S(1)}, u32[]{:S(2)}, u32[]{:S(2)}) collective-permute-start(bf16[128,1024]{1,0:T(8,128)(2,1)S(1)} %fusion.7), channel_id=1, source_target_pairs={{0,16},{4,20},{8,24},{12,28},{16,0},{20,4},{24,8},{28,12},{1,17},{... | collective-permute-start | bytes 786440 | tf_op jit(solution)/shard_map/ppermute | solution.py:414
  (29 other events, 314.0 us)

commit v2 on v1

--- a/solution.py
+++ b/solution.py
@@ -112,8 +112,9 @@
     refs = list(refs)
     places_ref = refs.pop(0)
     row_refs = [refs.pop(0) for _ in range(blocks)]
-    affine_ref, weight_ref, second_ref, active_ref, slope_ref = (refs.pop(0) for _ in range(5))
+    affine_ref, weight_ref, active_ref, slope_ref, result_ref = (refs.pop(0) for _ in range(5))
     arrival, rows_ref = refs.pop(-1), refs.pop(-1)
+    second_ref = refs.pop(0) if relative else result_ref
     size = row_refs[0].shape[0]
     for index, copy in enumerate(fetch(row_refs, rows_ref, arrival)):
         copy.wait()
@@ -123,7 +124,7 @@
             jnp.bfloat16
         )
     if relative:
-        copy_relative(places_ref, second_ref.shape[1] // 128, refs[0], second_ref)
+        copy_relative(places_ref, second_ref.shape[1] // 128, result_ref, second_ref)
     hidden = (
         lax.dot_general(
             second_ref[...], weight_ref[...], (NN, ((), ())), preferred_element_type=jnp.float32
@@ -145,20 +146,18 @@
     in_vmem = pl.BlockSpec(memory_space=pltpu.VMEM)
     narrow = jax.ShapeDtypeStruct((rows, width), jnp.bfloat16)
     shapes = [
-        narrow,
         jax.ShapeDtypeStruct((rows, units), jnp.bfloat16),
         jax.ShapeDtypeStruct((rows, units), jnp.float32),
+        narrow,
     ]
-    shapes += [narrow] if relative else []
+    scratch = pltpu.VMEM((rows, width), jnp.bfloat16)
     return pl.pallas_call(
         lambda *refs: front_body(*refs, blocks=len(pieces), relative=relative),
         in_specs=[in_smem] + piece_specs(pieces) + [in_vmem] * 2,
         out_specs=[in_vmem] * len(shapes),
         out_shape=shapes,
-        scratch_shapes=[
-            pltpu.VMEM((rows, width), jnp.bfloat16),
-            pltpu.SemaphoreType.DMA((len(pieces),)),
-        ],
+        scratch_shapes=[scratch] * (2 if relative else 1)
+        + [pltpu.SemaphoreType.DMA((len(pieces),))],
         compiler_params=pltpu.CompilerParams(vmem_limit_bytes=14 << 20),
         name="front",
     )(places, *pieces, affine, weight)
@@ -510,7 +509,9 @@
     affine = pack(affine, up_weight)
     groups = lax.axis_size("dp")
     relative = width // groups == 128
-    second_in, active, slope, *second_rel = front(places, token_pieces, affine, up_weight, relative)
+    active, slope, second_rel = front(
+        places, token_pieces, affine, up_weight, relative
+    )
     grad_rows_all, *grad_y = join(places, grad_pieces, relative)
     first_in, whole_normed, inv_std, bias_total, *rest = norm(
         places, token_pieces, affine, grad_rows_all, relative
@@ -519,12 +520,11 @@
     normed = whole_normed[:row_count]
     if relative:
         (grad_y,) = grad_y
-        (second_rel,) = second_rel
         first_rel, grad_z = rest
     else:
         grad_y = relative_blocks(grad_rows_all, "dp", y_first, 1)
         first_rel = relative_blocks(first_in, "dp", y_first, 1)
-        second_rel = relative_blocks(second_in, "dp", z_first, 1)
+        second_rel = relative_blocks(second_rel, "dp", z_first, 1)
         grad_z = relative_blocks(grad_rows_all, "dp", z_first, 1)
 
     def by_columns(left, right):

time: 156 us -> 156 us (level)
  no operation moved by 1% of the time
where the time goes in v2:
time: 156 us; the launch traced here: 155 us
  waiting for transfers between devices  67.9 us (44%)
  starting transfers between devices  29.1 us (19%)
  matrix products  24.1 us (15%)
  Pallas kernels  19.5 us (12%)
  local copies, waits for them, and re-layouts  8.86 us (6%)
  other arithmetic  4.6 us (3%)
    ppermute x25, waiting for transfers between devices, swap(): return lax.ppermute(array, axis, [(i, i ^ 1 << bit) for i in range(count)])  67.9 us
    ppermute x25, starting transfers between devices, swap(): return lax.ppermute(array, axis, [(i, i ^ 1 << bit) for i in range(count)])  29.1 us
    dot_general x17, matrix products, dot(): lax.dot_general(left, right, (dims, ((), ())), preferred_element_type=jnp...  24.1 us
    pallas_call x1, Pallas kernels, attention(): pl.pallas_call(attention_body, in_specs=[in_vmem] * 5 + [pl.BlockSpec(mem...  7.49 us
    unnamed x58, local copies, waits for them, and re-layouts  6.18 us
    pallas_call x1, Pallas kernels, front(): pl.pallas_call(lambda *refs: front_body(*refs, blocks=len(pieces), relati...  4.16 us
    add x5, other arithmetic, fold(): return lax.optimization_barrier(total) + arrived[-1][0]  3.23 us
    pallas_call x1, Pallas kernels, norm(): pl.pallas_call(lambda *refs: norm_body(*refs, blocks=len(pieces), relativ...  3.19 us
  transfers between devices with their start and end apart: 25, of which 12 were waited for; matrix products, arithmetic and copies ran while one was open for 19% of the time, Pallas kernels for 1%

profile of v2, /device:TPU:0, one launch (start us, length us, event | category | flops | bytes accessed | tf_op | source)
XLA Modules:
  0.0 155.2 jit_solution(638635781321494695)
XLA Ops:
  0.7 3.0 %collective-permute-start = (bf16[96,1024]{1,0:T(8,128)(2,1)}, bf16[96,1024]{1,0:T(8,128)(2,1)S(1)}, u32[]{:S(2)}, u32[]{:S(2)}) collective-permute-start(bf16[96,1024]{1,0:T(8,128)(2,1)} %refs_1_.5), channel_id=1, source_target_pairs={{0,2},{1,3},{2,0},{3,1},{4,6},{5,7},{6,4},{7,5},{8,10},{9,11},{10,... | collective-permute-start | bytes 589832 | tf_op jit(solution)/shard_map/ppermute | solution.py:413
  7.3 2.3 %collective-permute-done.refs_2_ = bf16[96,1024]{1,0:T(8,128)(2,1)S(1)} collective-permute-done((bf16[96,1024]{1,0:T(8,128)(2,1)}, bf16[96,1024]{1,0:T(8,128)(2,1)S(1)}, u32[]{:S(2)}, u32[]{:S(2)}) %collective-permute-start) | collective-permute-done | bytes 196640 | tf_op jit(solution)/shard_map/ppermute | solution.py:413
  9.7 3.4 %collective-permute-done.3.refs_2_ = bf16[96,1024]{1,0:T(8,128)(2,1)S(1)} collective-permute-done((bf16[96,1024]{1,0:T(8,128)(2,1)}, bf16[96,1024]{1,0:T(8,128)(2,1)S(1)}, u32[]{:S(2)}, u32[]{:S(2)}) %collective-permute-start.3) | collective-permute-done | bytes 196640 | tf_op jit(solution)/shard_map/ppermute | solution.py:413
  15.4 1.8 %join.1 = (bf16[384,1024]{1,0:T(8,128)(2,1)S(1)}, bf16[384,1024]{1,0:T(8,128)(2,1)S(1)}) custom-call(s32[16]{0:T(128)S(1)} %broadcast_xor_fusion.refs_0_, bf16[96,1024]{1,0:T(8,128)(2,1)S(1)} %copy-done.10, bf16[96,1024]{1,0:T(8,128)(2,1)S(1)} %collective-permute-done.3.refs_2_, bf16[96,1024]{1,0:T(8,128)(2,1)S(1)} %collective-permute-done.4.refs_3_, ...), custom_call_target="tpu_custom_call" | custom-call | tf_op jit(solution)/shard_map/join/pallas_call | solution.py:184
  17.3 4.2 %front.1 = (bf16[384,1024]{1,0:T(8,128)(2,1)S(1)}, f32[384,1024]{1,0:T(8,128)S(1)}, bf16[384,1024]{1,0:T(8,128)(2,1)S(1)}) custom-call(s32[16]{0:T(128)S(1)} %broadcast_xor_fusion.refs_0_, bf16[96,1024]{1,0:T(8,128)(2,1)S(1)} %copy-done.7, bf16[96,1024]{1,0:T(8,128)(2,1)S(1)} %collective-permute-done.refs_2_, ...), custom_call_target="tpu_custom_call" | custom-call | tf_op jit(solution)/shard_map/front/pallas_call | solution.py:154
  23.5 3.2 %norm.1 = (bf16[384,1024]{1,0:T(8,128)(2,1)S(1)}, f32[384,1024]{1,0:T(8,128)S(1)}, f32[96,1]{1,0:T(8,128)S(1)}, f32[1,1024]{1,0:T(1,128)S(1)}, bf16[384,1024]{1,...) custom-call(s32[16]{0:T(128)S(1)} %broadcast_xor_fusion.refs_0_, bf16[96,1024]{1,0:T(8,128)(2,1)S(1)} %copy-done.7, ...), custom_call_target="tpu_custom_call" | custom-call | tf_op jit(solution)/shard_map/norm/pallas_call | solution.py:231
  27.6 7.5 %attention.1 = (bf16[384,256]{1,0:T(8,128)(2,1)S(1)}, bf16[384,768]{1,0:T(8,128)(2,1)S(1)}, f32[1,768]{1,0:T(1,128)S(1)}) custom-call(bf16[384,1024]{1,0:T(8,128)(2,1)S(1)} %get-tuple-element.32.first_ref, bf16[1024,768]{1,0:T(8,128)(2,1)S(1)} %copy-done.3, f32[1,768]{1,0:T(1,128)S(1)} %broadcast_in_dim.2.bias_ref, ...), custom_call_target="tpu_custom_call" | custom-call | tf_op jit(solution)/shard_map/attention/pallas_call | solution.py:379
  35.1 2.9 %mix.1 = (f32[192,2048]{1,0:T(8,128)S(1)}, bf16[192,2048]{1,0:T(8,128)(2,1)S(1)}, f32[4,1024]{1,0:T(4,128)S(1)}) custom-call(bf16[384,768]{1,0:T(8,128)(2,1)S(1)} %get-tuple-element.33.d_joined_ref, bf16[1024,768]{1,0:T(8,128)(2,1)S(1)} %copy-done.3, bf16[384,1024]{1,0:T(8,128)(2,1)S(1)} %get-tuple-element.53.d_hidden_ref, bf16[1024,1024]{1,0:T(8,128)(2,1)S(1)} %copy-done.1, ...), custom_call_target="tpu_custom_call" | custom-call | tf_op jit(solution)/shard_map/mix/pallas_call | solution.py:285
  39.3 1.7 %collective-permute-start.9 = (f32[4096]{0:T(1024)S(1)}, f32[4096]{0:T(1024)S(1)}, u32[]{:S(2)}, u32[]{:S(2)}) collective-permute-start(f32[4096]{0:T(1024)S(1)} %fusion.35), channel_id=1, source_target_pairs={{0,2},{1,3},{2,0},{3,1},{4,6},{5,7},{6,4},{7,5},{8,10},{9,11},{10,... | collective-permute-start | bytes 49160 | tf_op jit(solution)/shard_map/ppermute | solution.py:413
  41.0 1.8 %convolution_convert_fusion = bf16[1024,512]{1,0:T(8,128)(2,1)} fusion(bf16[384,1024]{1,0:T(8,128)(2,1)S(1)} %get-tuple-element.37.active_ref, bf16[384,1024]{1,0:T(8,128)(2,1)S(1)} %get-tuple-element.47), kind=kOutput, calls=%fused_computation | convolution fusion | flops 403177472 | bytes 2228224 | tf_op jit(solution)/shard_map/dot_general | solution.py:464
  44.9 2.8 %convolution_convert_fusion.1 = bf16[512,1024]{1,0:T(8,128)(2,1)} fusion(bf16[384,1024]{1,0:T(8,128)(2,1)S(1)} %get-tuple-element.53.d_hidden_ref, bf16[384,1024]{1,0:T(8,128)(2,1)} %copy-done.15), kind=kOutput, calls=%fused_computation.1 | convolution fusion | flops 403177472 | bytes 2228224 | tf_op jit(solution)/shard_map/dot_general | solution.py:464
  49.3 19.3 %collective-permute-done.10 = f32[6912]{0:T(1024)S(1)} collective-permute-done((f32[6912]{0:T(1024)S(1)}, f32[6912]{0:T(1024)S(1)}, u32[]{:S(2)}, u32[]{:S(2)}) %collective-permute-start.10) | collective-permute-done | bytes 27680 | tf_op jit(solution)/shard_map/ppermute | solution.py:413
  68.6 2.6 %collective-permute-start.11 = (f32[6912]{0:T(1024)S(1)}, f32[6912]{0:T(1024)S(1)}, u32[]{:S(2)}, u32[]{:S(2)}) collective-permute-start(f32[6912]{0:T(1024)S(1)} %fusion.36), channel_id=1, source_target_pairs={{0,16},{4,20},{8,24},{12,28},{16,0},{20,4},{24,8},{28,12},{1,17},{... | collective-permute-start | bytes 82952 | tf_op jit(solution)/shard_map/ppermute | solution.py:413
  73.8 3.1 %collective-permute-start.12 = (f32[6912]{0:T(1024)S(1)}, f32[6912]{0:T(1024)S(1)}, u32[]{:S(2)}, u32[]{:S(2)}) collective-permute-start(f32[6912]{0:T(1024)S(1)} %add.130), channel_id=1, source_target_pairs={{0,8},{4,12},{8,0},{12,4},{16,24},{20,28},{24,16},{28,20},{1,9},{5... | collective-permute-start | bytes 82952 | tf_op jit(solution)/shard_map/ppermute | solution.py:413
  84.4 13.0 %collective-permute-done.17 = bf16[256,256]{1,0:T(8,128)(2,1)S(1)} collective-permute-done((bf16[256,256]{1,0:T(8,128)(2,1)S(1)}, bf16[256,256]{1,0:T(8,128)(2,1)S(1)}, u32[]{:S(2)}, u32[]{:S(2)}) %collective-permute-start.17) | collective-permute-done | bytes 131104 | tf_op jit(solution)/shard_map/ppermute | solution.py:413
  98.5 2.2 %collective-permute-start.18 = (bf16[256,128]{1,0:T(8,128)(2,1)S(1)}, bf16[256,128]{1,0:T(8,128)(2,1)S(1)}, u32[]{:S(2)}, u32[]{:S(2)}) collective-permute-start(bf16[256,128]{1,0:T(8,128)(2,1)S(1)} %fusion.15), channel_id=1, source_target_pairs={{0,16},{4,20},{8,24},{12,28},{16,0},{20,4},{24,8},{28,12},{1,17},{... | collective-permute-start | bytes 196616 | tf_op jit(solution)/shard_map/ppermute | solution.py:413
  101.9 2.6 %collective-permute-done.18 = bf16[256,128]{1,0:T(8,128)(2,1)S(1)} collective-permute-done((bf16[256,128]{1,0:T(8,128)(2,1)S(1)}, bf16[256,128]{1,0:T(8,128)(2,1)S(1)}, u32[]{:S(2)}, u32[]{:S(2)}) %collective-permute-start.18) | collective-permute-done | bytes 65568 | tf_op jit(solution)/shard_map/ppermute | solution.py:413
  109.6 2.0 %collective-permute-start.23 = (bf16[1024,256]{1,0:T(8,128)(2,1)S(1)}, bf16[1024,256]{1,0:T(8,128)(2,1)S(1)}, u32[]{:S(2)}, u32[]{:S(2)}) collective-permute-start(bf16[1024,256]{1,0:T(8,128)(2,1)S(1)} %fusion.1), channel_id=1, source_target_pairs={{0,8},{4,12},{8,0},{12,4},{16,24},{20,28},{24,16},{28,20},{1,9},{5... | collective-permute-start | bytes 1572872 | tf_op jit(solution)/shard_map/ppermute | solution.py:413
  113.1 1.6 %collective-permute-start.20 = (bf16[256,1024]{1,0:T(8,128)(2,1)S(1)}, bf16[256,1024]{1,0:T(8,128)(2,1)S(1)}, u32[]{:S(2)}, u32[]{:S(2)}) collective-permute-start(bf16[256,1024]{1,0:T(8,128)(2,1)S(1)} %fusion), channel_id=1, source_target_pairs={{0,4},{4,0},{8,12},{12,8},{16,20},{20,16},{24,28},{28,24},{1,5},{5... | collective-permute-start | bytes 1572872 | tf_op jit(solution)/shard_map/ppermute | solution.py:413
  114.7 6.0 %collective-permute-done.14 = bf16[256,768]{1,0:T(8,128)(2,1)S(1)} collective-permute-done((bf16[256,768]{1,0:T(8,128)(2,1)S(1)}, bf16[256,768]{1,0:T(8,128)(2,1)S(1)}, u32[]{:S(2)}, u32[]{:S(2)}) %collective-permute-start.14) | collective-permute-done | bytes 393248 | tf_op jit(solution)/shard_map/ppermute | solution.py:413
  125.0 12.5 %collective-permute-done.15 = bf16[128,768]{1,0:T(8,128)(2,1)S(1)} collective-permute-done((bf16[128,768]{1,0:T(8,128)(2,1)S(1)}, bf16[128,768]{1,0:T(8,128)(2,1)S(1)}, u32[]{:S(2)}, u32[]{:S(2)}) %collective-permute-start.15) | collective-permute-done | bytes 196640 | tf_op jit(solution)/shard_map/ppermute | solution.py:413
  141.0 3.0 %collective-permute-start.21 = (bf16[128,1024]{1,0:T(8,128)(2,1)S(1)}, bf16[128,1024]{1,0:T(8,128)(2,1)S(1)}, u32[]{:S(2)}, u32[]{:S(2)}) collective-permute-start(bf16[128,1024]{1,0:T(8,128)(2,1)S(1)} %fusion.7), channel_id=1, source_target_pairs={{0,16},{4,20},{8,24},{12,28},{16,0},{20,4},{24,8},{28,12},{1,17},{... | collective-permute-start | bytes 786440 | tf_op jit(solution)/shard_map/ppermute | solution.py:413
  146.6 4.3 %collective-permute-done.24 = bf16[1024,128]{1,0:T(8,128)(2,1)S(1)} collective-permute-done((bf16[1024,128]{1,0:T(8,128)(2,1)S(1)}, bf16[1024,128]{1,0:T(8,128)(2,1)S(1)}, u32[]{:S(2)}, u32[]{:S(2)}) %collective-permute-start.24) | collective-permute-done | bytes 262176 | tf_op jit(solution)/shard_map/ppermute | solution.py:413
  151.8 2.0 %collective-permute-done.21 = bf16[128,1024]{1,0:T(8,128)(2,1)S(1)} collective-permute-done((bf16[128,1024]{1,0:T(8,128)(2,1)S(1)}, bf16[128,1024]{1,0:T(8,128)(2,1)S(1)}, u32[]{:S(2)}, u32[]{:S(2)}) %collective-permute-start.21) | collective-permute-done | bytes 262176 | tf_op jit(solution)/shard_map/ppermute | solution.py:413
  (130 shorter events, 45.5 us)
Async XLA Ops:
  0.7 9.0 %collective-permute-start = (bf16[96,1024]{1,0:T(8,128)(2,1)}, bf16[96,1024]{1,0:T(8,128)(2,1)S(1)}, u32[]{:S(2)}, u32[]{:S(2)}) collective-permute-start(bf16[96,1024]{1,0:T(8,128)(2,1)} %refs_1_.5), channel_id=1, source_target_pairs={{0,2},{1,3},{2,0},{3,1},{4,6},{5,7},{6,4},{7,5},{8,10},{9,11},{10,... | collective-permute-start | bytes 589832 | tf_op jit(solution)/shard_map/ppermute | solution.py:413
  3.7 13.5 %collective-permute-start.1 = (bf16[96,1024]{1,0:T(8,128)(2,1)}, bf16[96,1024]{1,0:T(8,128)(2,1)S(1)}, u32[]{:S(2)}, u32[]{:S(2)}) collective-permute-start(bf16[96,1024]{1,0:T(8,128)(2,1)} %refs_1_.5), channel_id=1, source_target_pairs={{0,1},{1,0},{2,3},{3,2},{4,5},{5,4},{6,7},{7,6},{8,9},{9,8},{10,11... | collective-permute-start | bytes 589832 | tf_op jit(solution)/shard_map/ppermute | solution.py:413
  3.7 9.3 %collective-permute-start.3 = (bf16[96,1024]{1,0:T(8,128)(2,1)}, bf16[96,1024]{1,0:T(8,128)(2,1)S(1)}, u32[]{:S(2)}, u32[]{:S(2)}) collective-permute-start(bf16[96,1024]{1,0:T(8,128)(2,1)} %refs_1_.3), channel_id=1, source_target_pairs={{0,2},{1,3},{2,0},{3,1},{4,6},{5,7},{6,4},{7,5},{8,10},{9,11},{10,... | collective-permute-start | bytes 589832 | tf_op jit(solution)/shard_map/ppermute | solution.py:413
  3.9 9.2 %collective-permute-start.4 = (bf16[96,1024]{1,0:T(8,128)(2,1)}, bf16[96,1024]{1,0:T(8,128)(2,1)S(1)}, u32[]{:S(2)}, u32[]{:S(2)}) collective-permute-start(bf16[96,1024]{1,0:T(8,128)(2,1)} %refs_1_.3), channel_id=1, source_target_pairs={{0,1},{1,0},{2,3},{3,2},{4,5},{5,4},{6,7},{7,6},{8,9},{9,8},{10,11... | collective-permute-start | bytes 589832 | tf_op jit(solution)/shard_map/ppermute | solution.py:413
  9.7 7.6 %collective-permute-start.2 = (bf16[96,1024]{1,0:T(8,128)(2,1)S(1)}, bf16[96,1024]{1,0:T(8,128)(2,1)S(1)}, u32[]{:S(2)}, u32[]{:S(2)}) collective-permute-start(bf16[96,1024]{1,0:T(8,128)(2,1)S(1)} %collective-permute-done.refs_2_), channel_id=1, source_target_pairs={{0,1},{1,0},{2,3},{3,2},{4,5},{5,4},{6,7},{7,6},{8,9},{9,8},{10,11... | collective-permute-start | bytes 589832 | tf_op jit(solution)/shard_map/ppermute | solution.py:413
  13.0 1.4 collective-permute-start.5
  39.3 5.1 %collective-permute-start.9 = (f32[4096]{0:T(1024)S(1)}, f32[4096]{0:T(1024)S(1)}, u32[]{:S(2)}, u32[]{:S(2)}) collective-permute-start(f32[4096]{0:T(1024)S(1)} %fusion.35), channel_id=1, source_target_pairs={{0,2},{1,3},{2,0},{3,1},{4,6},{5,7},{6,4},{7,5},{8,10},{9,11},{10,... | collective-permute-start | bytes 49160 | tf_op jit(solution)/shard_map/ppermute | solution.py:413
  42.8 64.8 %collective-permute-start.22 = (bf16[1024,512]{1,0:T(8,128)(2,1)}, bf16[1024,512]{1,0:T(8,128)(2,1)}, u32[]{:S(2)}, u32[]{:S(2)}) collective-permute-start(bf16[1024,512]{1,0:T(8,128)(2,1)} %convolution_convert_fusion), channel_id=1, source_target_pairs={{0,4},{4,0},{8,12},{12,8},{16,20},{20,16},{24,28},{28,24},{1,5},{5... | collective-permute-start | bytes 3145736 | tf_op jit(solution)/shard_map/ppermute | solution.py:413
  44.4 24.2 %collective-permute-start.10 = (f32[6912]{0:T(1024)S(1)}, f32[6912]{0:T(1024)S(1)}, u32[]{:S(2)}, u32[]{:S(2)}) collective-permute-start(f32[6912]{0:T(1024)S(1)} %pad_maximum_fusion), channel_id=1, source_target_pairs={{0,4},{4,0},{8,12},{12,8},{16,20},{20,16},{24,28},{28,24},{1,5},{5... | collective-permute-start | bytes 82952 | tf_op jit(solution)/shard_map/ppermute | solution.py:413
  47.7 63.9 %collective-permute-start.19 = (bf16[512,1024]{1,0:T(8,128)(2,1)}, bf16[512,1024]{1,0:T(8,128)(2,1)}, u32[]{:S(2)}, u32[]{:S(2)}) collective-permute-start(bf16[512,1024]{1,0:T(8,128)(2,1)} %convolution_convert_fusion.1), channel_id=1, source_target_pairs={{0,8},{4,12},{8,0},{12,4},{16,24},{20,28},{24,16},{28,20},{1,9},{5... | collective-permute-start | bytes 3145736 | tf_op jit(solution)/shard_map/ppermute | solution.py:413
  68.6 5.2 %collective-permute-start.11 = (f32[6912]{0:T(1024)S(1)}, f32[6912]{0:T(1024)S(1)}, u32[]{:S(2)}, u32[]{:S(2)}) collective-permute-start(f32[6912]{0:T(1024)S(1)} %fusion.36), channel_id=1, source_target_pairs={{0,16},{4,20},{8,24},{12,28},{16,0},{20,4},{24,8},{28,12},{1,17},{... | collective-permute-start | bytes 82952 | tf_op jit(solution)/shard_map/ppermute | solution.py:413
  72.2 7.9 %collective-permute-start.16 = (bf16[256,512]{1,0:T(8,128)(2,1)}, bf16[256,512]{1,0:T(8,128)(2,1)}, u32[]{:S(2)}, u32[]{:S(2)}) collective-permute-start(bf16[256,512]{1,0:T(8,128)(2,1)} %convolution_convert_fusion.3), channel_id=1, source_target_pairs={{0,8},{4,12},{8,0},{12,4},{16,24},{20,28},{24,16},{28,20},{1,9},{5... | collective-permute-start | bytes 786440 | tf_op jit(solution)/shard_map/ppermute | solution.py:413
  73.8 6.3 %collective-permute-start.12 = (f32[6912]{0:T(1024)S(1)}, f32[6912]{0:T(1024)S(1)}, u32[]{:S(2)}, u32[]{:S(2)}) collective-permute-start(f32[6912]{0:T(1024)S(1)} %add.130), channel_id=1, source_target_pairs={{0,8},{4,12},{8,0},{12,4},{16,24},{20,28},{24,16},{28,20},{1,9},{5... | collective-permute-start | bytes 82952 | tf_op jit(solution)/shard_map/ppermute | solution.py:413
  78.4 26.8 %collective-permute-start.13 = (bf16[512,768]{1,0:T(8,128)(2,1)}, bf16[512,768]{1,0:T(8,128)(2,1)}, u32[]{:S(2)}, u32[]{:S(2)}) collective-permute-start(bf16[512,768]{1,0:T(8,128)(2,1)} %convolution_convert_fusion.2), channel_id=1, source_target_pairs={{0,4},{4,0},{8,12},{12,8},{16,20},{20,16},{24,28},{28,24},{1,5},{5... | collective-permute-start | bytes 2359304 | tf_op jit(solution)/shard_map/ppermute | solution.py:413
  80.1 26.7 %collective-permute-start.6 = (bf16[192,2048]{1,0:T(8,128)(2,1)}, bf16[192,2048]{1,0:T(8,128)(2,1)S(1)}, u32[]{:S(2)}, u32[]{:S(2)}) collective-permute-start(bf16[192,2048]{1,0:T(8,128)(2,1)} %copy-done.22), channel_id=1, source_target_pairs={{0,1},{1,0},{2,3},{3,2},{4,5},{5,4},{6,7},{7,6},{8,9},{9,8},{10,11... | collective-permute-start | bytes 2359304 | tf_op jit(solution)/shard_map/ppermute | solution.py:413
  81.7 15.7 %collective-permute-start.17 = (bf16[256,256]{1,0:T(8,128)(2,1)S(1)}, bf16[256,256]{1,0:T(8,128)(2,1)S(1)}, u32[]{:S(2)}, u32[]{:S(2)}) collective-permute-start(bf16[256,256]{1,0:T(8,128)(2,1)S(1)} %fusion.12), channel_id=1, source_target_pairs={{0,4},{4,0},{8,12},{12,8},{16,20},{20,16},{24,28},{28,24},{1,5},{5... | collective-permute-start | bytes 393224 | tf_op jit(solution)/shard_map/ppermute | solution.py:413
  98.5 5.9 %collective-permute-start.18 = (bf16[256,128]{1,0:T(8,128)(2,1)S(1)}, bf16[256,128]{1,0:T(8,128)(2,1)S(1)}, u32[]{:S(2)}, u32[]{:S(2)}) collective-permute-start(bf16[256,128]{1,0:T(8,128)(2,1)S(1)} %fusion.15), channel_id=1, source_target_pairs={{0,16},{4,20},{8,24},{12,28},{16,0},{20,4},{24,8},{28,12},{1,17},{... | collective-permute-start | bytes 196616 | tf_op jit(solution)/shard_map/ppermute | solution.py:413
  106.5 14.2 %collective-permute-start.14 = (bf16[256,768]{1,0:T(8,128)(2,1)S(1)}, bf16[256,768]{1,0:T(8,128)(2,1)S(1)}, u32[]{:S(2)}, u32[]{:S(2)}) collective-permute-start(bf16[256,768]{1,0:T(8,128)(2,1)S(1)} %fusion.2), channel_id=1, source_target_pairs={{0,8},{4,12},{8,0},{12,4},{16,24},{20,28},{24,16},{28,20},{1,9},{5... | collective-permute-start | bytes 1179656 | tf_op jit(solution)/shard_map/ppermute | solution.py:413
  106.9 15.1 %collective-permute-start.7 = (bf16[96,2048]{1,0:T(8,128)(2,1)S(1)}, bf16[96,2048]{1,0:T(8,128)(2,1)S(1)}, u32[]{:S(2)}, u32[]{:S(2)}) collective-permute-start(bf16[96,2048]{1,0:T(8,128)(2,1)S(1)} %get-tuple-element.50), channel_id=1, source_target_pairs={{0,2},{1,3},{2,0},{3,1},{4,6},{5,7},{6,4},{7,5},{8,10},{9,11},{10,... | collective-permute-start | bytes 1179656 | tf_op jit(solution)/shard_map/ppermute | solution.py:413
  109.6 28.6 %collective-permute-start.23 = (bf16[1024,256]{1,0:T(8,128)(2,1)S(1)}, bf16[1024,256]{1,0:T(8,128)(2,1)S(1)}, u32[]{:S(2)}, u32[]{:S(2)}) collective-permute-start(bf16[1024,256]{1,0:T(8,128)(2,1)S(1)} %fusion.1), channel_id=1, source_target_pairs={{0,8},{4,12},{8,0},{12,4},{16,24},{20,28},{24,16},{28,20},{1,9},{5... | collective-permute-start | bytes 1572872 | tf_op jit(solution)/shard_map/ppermute | solution.py:413
  113.1 26.6 %collective-permute-start.20 = (bf16[256,1024]{1,0:T(8,128)(2,1)S(1)}, bf16[256,1024]{1,0:T(8,128)(2,1)S(1)}, u32[]{:S(2)}, u32[]{:S(2)}) collective-permute-start(bf16[256,1024]{1,0:T(8,128)(2,1)S(1)} %fusion), channel_id=1, source_target_pairs={{0,4},{4,0},{8,12},{12,8},{16,20},{20,16},{24,28},{28,24},{1,5},{5... | collective-permute-start | bytes 1572872 | tf_op jit(solution)/shard_map/ppermute | solution.py:413
  122.0 15.5 %collective-permute-start.15 = (bf16[128,768]{1,0:T(8,128)(2,1)S(1)}, bf16[128,768]{1,0:T(8,128)(2,1)S(1)}, u32[]{:S(2)}, u32[]{:S(2)}) collective-permute-start(bf16[128,768]{1,0:T(8,128)(2,1)S(1)} %fusion.11), channel_id=1, source_target_pairs={{0,16},{4,20},{8,24},{12,28},{16,0},{20,4},{24,8},{28,12},{1,17},{... | collective-permute-start | bytes 589832 | tf_op jit(solution)/shard_map/ppermute | solution.py:413
  139.6 11.3 %collective-permute-start.24 = (bf16[1024,128]{1,0:T(8,128)(2,1)S(1)}, bf16[1024,128]{1,0:T(8,128)(2,1)S(1)}, u32[]{:S(2)}, u32[]{:S(2)}) collective-permute-start(bf16[1024,128]{1,0:T(8,128)(2,1)S(1)} %fusion.8), channel_id=1, source_target_pairs={{0,16},{4,20},{8,24},{12,28},{16,0},{20,4},{24,8},{28,12},{1,17},{... | collective-permute-start | bytes 786440 | tf_op jit(solution)/shard_map/ppermute | solution.py:413
  141.0 12.8 %collective-permute-start.21 = (bf16[128,1024]{1,0:T(8,128)(2,1)S(1)}, bf16[128,1024]{1,0:T(8,128)(2,1)S(1)}, u32[]{:S(2)}, u32[]{:S(2)}) collective-permute-start(bf16[128,1024]{1,0:T(8,128)(2,1)S(1)} %fusion.7), channel_id=1, source_target_pairs={{0,16},{4,20},{8,24},{12,28},{16,0},{20,4},{24,8},{28,12},{1,17},{... | collective-permute-start | bytes 786440 | tf_op jit(solution)/shard_map/ppermute | solution.py:413
  (29 other events, 314.1 us)
